TPU v7x, 256 devices: a whole 4x4x8 slice. The times are simulated.
256 devices in a mesh: tracer: 2 (over core), dev: 128 (over z, y, x).
Axes of the slice: x: 4, y: 4, z: 8, core: 2. Of those that a mesh axis runs over, the one named last changes fastest.
Arguments:
- coeffs: bfloat16 [2, 256, 256, 2047], P('tracer', 'dev'), may hold values from -6 to 6
- bessel: bfloat16 [2, 1536, 512, 256], P('tracer', 'dev'), may hold values from -0.375 to 0.375
- azimuthal_order_slots: int32 [128], replicated, may hold values from 0 to 1524, as said below
Outputs:
- cross: float32 [2, 768, 512, 512], P('tracer', 'dev')
Inputs may be any that keep to these rules, and one draw needn't show every extreme that they name: `azimuthal_order_slots`: the 128 values are exactly the multiples k * (12) for k = 0 .. 127, each once, in an order drawn from the seed.
All inputs are finite; a program needn't handle non-finite values.
Results may differ from a plain program's by a relative error of at most 0.008.
Values may be sent and summed in bfloat16 or wider, within the bound.
No kernel may reach another device: no remote copies, remote signals or barrier semaphores. Data moves between devices by JAX's collectives and lax.ppermute only.
A program may use at most 64 MiB of HBM per device.

v0:
```python
import jax
import jax.numpy as jnp
from jax import lax
from jax.sharding import PartitionSpec as P

NSIDE = 512
CYCLES = 2047
LMAX = 1536
SHELLS = 256
M_DEV = 1
LB = 128


rescale_limit = 10000000000.0


def swapped(value, axis, apart):
    mask = 2**apart
    pairs = [(source, source ^ mask) for source in range(lax.axis_size(axis))]
    return lax.ppermute(value, axis, pairs)


def cycle_geometry():
    cycle_number = jnp.arange(1, CYCLES + 1, dtype=jnp.float32)
    nside_float = jnp.float32(NSIDE)
    folded = jnp.minimum(cycle_number, 4.0 * nside_float - cycle_number)
    polar_cycle = folded < nside_float
    polar_gap = folded * folded / (3.0 * nside_float * nside_float)
    equator_height = 4.0 / 3.0 - 2.0 * folded / (3.0 * nside_float)
    cycle_height = jnp.where(polar_cycle, 1.0 - polar_gap, equator_height)
    height_gap = jnp.where(polar_cycle, polar_gap, 1.0 - equator_height)
    sine_cycle = jnp.sqrt(height_gap * (1.0 + cycle_height))
    cosine_latitude = jnp.where(cycle_number <= 2.0 * nside_float, cycle_height, -cycle_height)
    pixels = jnp.where(polar_cycle, 4.0 * folded, 4.0 * nside_float)
    weight = jnp.sqrt(jnp.pi * pixels / (3.0 * nside_float * nside_float))
    return (cosine_latitude, sine_cycle, weight)


def legendre_seed(orders, sine_cycle):
    counter = jnp.arange(1, LMAX + 1, dtype=jnp.float32)
    log_terms = jnp.log1p(-0.5 / counter)
    partial_sum = jnp.sum(
        jnp.where(counter[None, :] <= orders[:, None], log_terms[None, :], 0.0), axis=1
    )
    head = 0.5 * jnp.log((2.0 * orders + 1.0) / (4.0 * jnp.pi)) + 0.5 * partial_sum
    return head[:, None] + orders[:, None] * jnp.log(sine_cycle)[None, :]


def recurrence_step(carried, degree, orders, cosine_latitude, seed_log):
    previous, current, log_scale = carried
    order_col = orders[:, None]
    alpha_coef = jnp.sqrt(
        jnp.maximum(4.0 * degree * degree - 1.0, 1.0)
        / jnp.maximum(degree * degree - order_col * order_col, 1.0)
    )
    degree_below = degree - 1.0
    beta_coef = jnp.sqrt(
        jnp.maximum(degree_below * degree_below - order_col * order_col, 0.0)
        / jnp.maximum(4.0 * degree_below * degree_below - 1.0, 1.0)
    )
    starting_degree = degree == order_col
    updated = jnp.where(
        starting_degree,
        1.0,
        alpha_coef * (cosine_latitude[None, :] * current - beta_coef * previous),
    )
    previous = jnp.where(starting_degree, 0.0, current)
    log_scale = jnp.where(starting_degree, seed_log, log_scale)
    table_value = jnp.where(degree >= order_col, updated * jnp.exp(log_scale), 0.0)
    largest = jnp.maximum(jnp.abs(updated), jnp.abs(previous))
    oversized = largest > rescale_limit
    factor = jnp.where(oversized, 1.0 / jnp.maximum(largest, 1.0), 1.0)
    log_scale = log_scale + jnp.where(oversized, jnp.log(jnp.maximum(largest, 1.0)), 0.0)
    return ((previous * factor, updated * factor, log_scale), table_value)


def legendre_block(carried, first_degree, orders, cosine_latitude, seed_log, weight):

    def advance(inner_state, offset):
        degree = (first_degree + offset).astype(jnp.float32)
        return recurrence_step(inner_state, degree, orders, cosine_latitude, seed_log)

    carried, values = lax.scan(advance, carried, jnp.arange(LB, dtype=jnp.int32), unroll=8)
    return (carried, (values * weight[None, None, :]).astype(jnp.bfloat16))


def per_device(coeffs, bessel, azimuthal_order_slots):
    cosine_latitude, sine_cycle, weight = cycle_geometry()
    device = lax.axis_index("dev")
    local_orders = lax.dynamic_slice_in_dim(azimuthal_order_slots, device * M_DEV, M_DEV)
    orders = local_orders.astype(jnp.float32)
    seed_log = legendre_seed(orders, sine_cycle)
    regrouped = lax.all_to_all(coeffs[0], "dev", split_axis=1, concat_axis=0, tiled=True)
    grouped_coefficients = regrouped.reshape(SHELLS, M_DEV, 2, CYCLES)
    zero_rows = jnp.zeros((M_DEV, CYCLES), jnp.float32)
    harmonic = jnp.zeros((M_DEV, 2, LMAX, SHELLS), jnp.bfloat16)

    def fill_block(block_index, packed):
        carried, harmonic_now = packed
        carried, weighted_harmonics = legendre_block(
            carried, block_index * LB, orders, cosine_latitude, seed_log, weight
        )
        block_terms = jnp.einsum(
            "jhq,vhyq->hyjv",
            weighted_harmonics,
            grouped_coefficients,
            preferred_element_type=jnp.float32,
        ).astype(jnp.bfloat16)
        harmonic_now = lax.dynamic_update_slice_in_dim(
            harmonic_now, block_terms, block_index * LB, 2
        )
        return (carried, harmonic_now)

    first_block = jnp.min(local_orders) // LB
    final_state, harmonic = lax.fori_loop(
        first_block, LMAX // LB, fill_block, ((zero_rows, zero_rows, zero_rows), harmonic)
    )
    by_degree = lax.all_to_all(
        harmonic.reshape(2 * M_DEV, LMAX, SHELLS), "dev", split_axis=1, concat_axis=0, tiled=True
    )
    radial = jnp.einsum(
        "cls,lks->lck", by_degree, bessel[0], preferred_element_type=jnp.float32
    ).astype(jnp.bfloat16)
    degrees_here = by_degree.shape[1]
    half_depth = degrees_here // 2
    tracer_id = lax.axis_index("tracer")
    own_half = lax.dynamic_slice_in_dim(radial, tracer_id * half_depth, half_depth, 0)
    partner_all = swapped(radial, "tracer", 0)
    other_half = lax.dynamic_slice_in_dim(partner_all, tracer_id * half_depth, half_depth, 0)
    leading = jnp.where(tracer_id == 0, own_half, other_half)
    trailing = jnp.where(tracer_id == 0, other_half, own_half)
    degree_values = (
        device * degrees_here + tracer_id * half_depth + jnp.arange(half_depth, dtype=jnp.int32)
    )
    mode_tallies = jnp.sum(
        (azimuthal_order_slots[None, :] <= degree_values[:, None]).astype(jnp.int32), axis=1
    )
    factor = 1.0 / jnp.sqrt(2.0 * mode_tallies.astype(jnp.float32))
    cross_power_spectrum = (
        jnp.einsum("lck,lcj->lkj", leading, trailing, preferred_element_type=jnp.float32)
        * factor[:, None, None]
    )
    return cross_power_spectrum[None]


def solution(mesh):
    placed = (P("tracer", "dev", None, None), P("tracer", "dev", None, None), P())
    return jax.shard_map(
        per_device,
        mesh=mesh,
        in_specs=placed,
        out_specs=P("tracer", "dev", None, None),
        check_vma=False,
    )
```

profile of v0, /device:TPU:1, one launch (start us, length us, event | category | flops | bytes accessed | tf_op | source)
XLA Modules:
  0.0 1833.7 jit_solution(6060796921105758422)
XLA Ops:
  0.0 8.6 copy.30
  8.6 17.0 all-to-all-start
  30.1 44.9 %all-to-all-done = bf16[2,256,2047]{2,0,1:T(2,128)(2,1)} async-done(((bf16[2,256,2047]{2,0,1:T(2,128)(2,1)}), bf16[2,256,2047]{2,0,1:T(2,128)(2,1)}, u32[]{:S(2)}, u32[]{:S(2)}) %all-to-all-start) | async-done | bytes 2096160 | tf_op jit(solution)/shard_map/all_to_all | solution.py:93
  75.0 4.1 copy.31
  79.1 2.2 copy.32
  81.3 2.2 broadcast_in_dim.397.clone
  83.5 1116.8 %while.58 = (s32[]{:T(128)}, f32[1,2047]{1,0:T(1,128)S(1)}, f32[1,2047]{1,0:T(1,128)S(1)}, f32[1,2047]{1,0:T(1,128)S(1)}, bf16[1,2,1536,256]{3,1,2,0:T(2,128)(2,...) while((s32[]{:T(128)}, f32[1,2047]{1,0:T(1,128)S(1)}, ...), condition=%wide.region_4.5_spmd.clone.clone, body=%wide.region_1.4_spmd.clone.clone.sunk | while | flops 269375424 | bytes 4482716 | solution.py:115
  83.6 135.9 %while.59 = (s32[]{:T(128)}, f32[1,2047]{1,0:T(1,128)S(1)}, f32[1,2047]{1,0:T(1,128)S(1)}, f32[1,2047]{1,0:T(1,128)S(1)}, f32[16,8,1,2047]{3,1,0,2:T(8,128)}, /*...) while((s32[]{:T(128)}, f32[1,2047]{1,0:T(1,128)S(1)}, ...), condition=%wide.region_3.3_spmd.clone, body=%wide.region_2.2_spmd.clone.sunk | while | flops 407522 | bytes 911661 | solution.py:83
  219.5 2.7 fusion.62
  223.2 135.9 %while.59 = (s32[]{:T(128)}, f32[1,2047]{1,0:T(1,128)S(1)}, f32[1,2047]{1,0:T(1,128)S(1)}, f32[1,2047]{1,0:T(1,128)S(1)}, f32[16,8,1,2047]{3,1,0,2:T(8,128)}, /*...) while((s32[]{:T(128)}, f32[1,2047]{1,0:T(1,128)S(1)}, ...), condition=%wide.region_3.3_spmd.clone, body=%wide.region_2.2_spmd.clone.sunk | while | flops 407522 | bytes 911661 | solution.py:83
  359.1 2.7 fusion.62
  362.8 135.9 %while.59 = (s32[]{:T(128)}, f32[1,2047]{1,0:T(1,128)S(1)}, f32[1,2047]{1,0:T(1,128)S(1)}, f32[1,2047]{1,0:T(1,128)S(1)}, f32[16,8,1,2047]{3,1,0,2:T(8,128)}, /*...) while((s32[]{:T(128)}, f32[1,2047]{1,0:T(1,128)S(1)}, ...), condition=%wide.region_3.3_spmd.clone, body=%wide.region_2.2_spmd.clone.sunk | while | flops 407522 | bytes 911661 | solution.py:83
  498.7 2.7 fusion.62
  501.5 0.8 copy_dynamic-update-slice_fusion.4
  502.4 135.9 %while.59 = (s32[]{:T(128)}, f32[1,2047]{1,0:T(1,128)S(1)}, f32[1,2047]{1,0:T(1,128)S(1)}, f32[1,2047]{1,0:T(1,128)S(1)}, f32[16,8,1,2047]{3,1,0,2:T(8,128)}, /*...) while((s32[]{:T(128)}, f32[1,2047]{1,0:T(1,128)S(1)}, ...), condition=%wide.region_3.3_spmd.clone, body=%wide.region_2.2_spmd.clone.sunk | while | flops 407522 | bytes 911661 | solution.py:83
  638.3 2.7 fusion.62
  642.0 135.9 %while.59 = (s32[]{:T(128)}, f32[1,2047]{1,0:T(1,128)S(1)}, f32[1,2047]{1,0:T(1,128)S(1)}, f32[1,2047]{1,0:T(1,128)S(1)}, f32[16,8,1,2047]{3,1,0,2:T(8,128)}, /*...) while((s32[]{:T(128)}, f32[1,2047]{1,0:T(1,128)S(1)}, ...), condition=%wide.region_3.3_spmd.clone, body=%wide.region_2.2_spmd.clone.sunk | while | flops 407522 | bytes 911661 | solution.py:83
  777.9 2.7 fusion.62
  781.6 135.9 %while.59 = (s32[]{:T(128)}, f32[1,2047]{1,0:T(1,128)S(1)}, f32[1,2047]{1,0:T(1,128)S(1)}, f32[1,2047]{1,0:T(1,128)S(1)}, f32[16,8,1,2047]{3,1,0,2:T(8,128)}, /*...) while((s32[]{:T(128)}, f32[1,2047]{1,0:T(1,128)S(1)}, ...), condition=%wide.region_3.3_spmd.clone, body=%wide.region_2.2_spmd.clone.sunk | while | flops 407522 | bytes 911661 | solution.py:83
  917.5 2.7 fusion.62
  921.2 135.9 %while.59 = (s32[]{:T(128)}, f32[1,2047]{1,0:T(1,128)S(1)}, f32[1,2047]{1,0:T(1,128)S(1)}, f32[1,2047]{1,0:T(1,128)S(1)}, f32[16,8,1,2047]{3,1,0,2:T(8,128)}, /*...) while((s32[]{:T(128)}, f32[1,2047]{1,0:T(1,128)S(1)}, ...), condition=%wide.region_3.3_spmd.clone, body=%wide.region_2.2_spmd.clone.sunk | while | flops 407522 | bytes 911661 | solution.py:83
  1057.2 2.7 fusion.62
  1060.8 135.9 %while.59 = (s32[]{:T(128)}, f32[1,2047]{1,0:T(1,128)S(1)}, f32[1,2047]{1,0:T(1,128)S(1)}, f32[1,2047]{1,0:T(1,128)S(1)}, f32[16,8,1,2047]{3,1,0,2:T(8,128)}, /*...) while((s32[]{:T(128)}, f32[1,2047]{1,0:T(1,128)S(1)}, ...), condition=%wide.region_3.3_spmd.clone, body=%wide.region_2.2_spmd.clone.sunk | while | flops 407522 | bytes 911661 | solution.py:83
  1196.7 2.7 fusion.62
  1199.5 0.8 copy_dynamic-update-slice_fusion.4
  1200.3 606.7 %all_to_all.33 = bf16[2,1536,256]{2,0,1:T(2,128)(2,1)S(1)} all-to-all(bf16[2,1536,256]{2,0,1:T(2,128)(2,1)} %bitcast.356), channel_id=1, replica_groups=mesh['tracer'=2,'dev'=128] {'dev'}, dimensions={1} | all-to-all | bytes 3145728 | tf_op jit(solution)/shard_map/all_to_all | solution.py:118
  1807.0 2.6 copy.34
  1809.6 3.6 all_to_all.30
  1813.2 4.0 fusion.40
  1817.3 3.7 collective-permute-start
  1821.2 5.4 collective-permute-done
  1826.6 7.1 multiply_bitcast_fusion
  (1850 shorter events, 275.8 us)
Async XLA Ops:
  0.0 1813.2 %copy-start = (bf16[1,12,512,256]{3,2,1,0:T(8,128)(2,1)S(1)}, bf16[1,12,512,256]{3,2,1,0:T(8,128)(2,1)}, u32[]{:S(2)}) copy-start(bf16[1,12,512,256]{3,2,1,0:T(8,128)(2,1)} %param.8) | copy-start | bytes 9437188
  8.6 17.0 copy-start.1
  8.6 66.4 %all-to-all-start = ((bf16[2,256,2047]{2,0,1:T(2,128)(2,1)}), bf16[2,256,2047]{2,0,1:T(2,128)(2,1)}, u32[]{:S(2)}, u32[]{:S(2)}) async-start(bf16[2,256,2047]{2,0,1:T(2,128)(2,1)} %bitcast.354), calls=%async_computation | async-start | bytes 4194304 | tf_op jit(solution)/shard_map/all_to_all | solution.py:93
  1817.3 9.4 collective-permute-start
where the time goes:
time: 1850 us; the launch traced here: 1830 us
  loops' own time  819 us (44%)
  blocking collectives  607 us (33%)
  local copies, waits for them, and re-layouts  203 us (11%)
  other arithmetic  97.7 us (5%)
  waiting for transfers between devices  50.3 us (3%)
  matrix products  33 us (2%)
  starting transfers between devices  20.7 us (1%)
    another operation x8, loops' own time, legendre_block(): lax.scan(advance, carried, jnp.arange(LB, dtype=jnp.int32), unroll=8)  819 us
    all_to_all x1, blocking collectives, per_device(): lax.all_to_all(harmonic.reshape(2 * M_DEV, LMAX, SHELLS), 'dev', split_ax...  607 us
    dynamic_update_slice x128, local copies, waits for them, and re-layouts, legendre_block(): lax.scan(advance, carried, jnp.arange(LB, dtype=jnp.int32), unroll=8)  83.5 us
    slice x128, local copies, waits for them, and re-layouts, legendre_block(): lax.scan(advance, carried, jnp.arange(LB, dtype=jnp.int32), unroll=8)  80 us
    while x896, other arithmetic  74 us
    all_to_all x1, waiting for transfers between devices, per_device(): lax.all_to_all(coeffs[0], 'dev', split_axis=1, concat_axis=0, tiled=True)  44.9 us
  transfers between devices with their start and end apart: 2, of which 2 were waited for; matrix products, arithmetic and copies ran while one was open for 0% of the time, Pallas kernels for 0%

commit v1 on v0

v1 whole, which is shorter than its diff:
```python
import jax
import jax.numpy as jnp
from jax import lax
from jax.experimental import pallas as pl
from jax.experimental.pallas import tpu as pltpu
from jax.sharding import PartitionSpec as P

NSIDE = 512
CYCLES = 2047
LMAX = 1536
STRIDE = 12
HALF = 1024
PLANE = 16
PLANES = 8
OWNERS = 128
TABLE = LMAX + 16
BLOCK_ROWS = 6 * PLANE
STEP_LOG2 = 64.0
STEP_LN_HIGH = 44.359375
STEP_LN_LOW = 0.0020445558364884
BIG = 2.0**32
SHRINK = 2.0**-64


def half_rows(j):
    return BLOCK_ROWS * (PLANES - j)


def table_base(j):
    return sum(2 * half_rows(i) for i in range(j))


TABLE_ROWS = table_base(PLANES)


def order_index(j, place):
    flip = lax.rem(j, 2)
    return PLANE * j + jnp.where(flip == 0, place, PLANE - 1 - place)


def fold_kernel(slots_ref, coef_ref, out_ref):
    x = coef_ref[0]
    row = lax.broadcasted_iota(jnp.int32, (256, 256), 0)
    col = lax.broadcasted_iota(jnp.int32, (256, 256), 1)
    group = row // 16
    j = (row % 16) // 2
    place = jnp.where(j % 2 == 0, group, PLANE - 1 - group)
    wanted = STRIDE * (PLANE * j + place)
    hit = jnp.logical_and(slots_ref[...] == wanted, row % 2 == col % 2)
    pick = jnp.where(hit, 1.0, 0.0).astype(jnp.bfloat16)
    south = x[:, HALF:].astype(jnp.float32)
    lane = lax.broadcasted_iota(jnp.int32, south.shape, 1)
    south = jnp.where(lane < HALF - 1, south, 0.0).astype(jnp.bfloat16)
    north = jnp.dot(pick, x[:, :HALF], preferred_element_type=jnp.float32)
    south = jnp.dot(pick, south, preferred_element_type=jnp.float32).astype(jnp.bfloat16)
    back_row = lax.broadcasted_iota(jnp.int32, (256, 128), 0)
    back_col = lax.broadcasted_iota(jnp.int32, (256, 128), 1)
    back = jnp.where(back_row + back_col == 254, 1.0, 0.0).astype(jnp.bfloat16)
    for b in range(8):
        if b < 7:
            mirrored = jnp.dot(
                south[:, 128 * (6 - b) : 128 * (8 - b)], back, preferred_element_type=jnp.float32
            )
        else:
            mirrored = jnp.dot(south[:, :128], back[128:], preferred_element_type=jnp.float32)
        here = north[:, 128 * b : 128 * (b + 1)]
        even = (here + mirrored).astype(jnp.bfloat16)
        odd = (here - mirrored).astype(jnp.bfloat16)
        out_ref[:, 0, :, 128 * b : 128 * (b + 1)] = even.reshape(16, 16, 128)
        out_ref[:, 0, :, HALF + 128 * b : HALF + 128 * (b + 1)] = odd.reshape(16, 16, 128)


def fold_coefficients(slots_pair, coeffs):
    return pl.pallas_call(
        fold_kernel,
        grid=(2,),
        in_specs=[
            pl.BlockSpec((1, 256), lambda s: (0, 0)),
            pl.BlockSpec((1, 256, 2 * HALF), lambda s: (s, 0, 0)),
        ],
        out_specs=pl.BlockSpec((16, 1, 16, 2 * HALF), lambda s: (0, s, 0, 0)),
        out_shape=jax.ShapeDtypeStruct((16, 2, 16, 2 * HALF), jnp.bfloat16),
        compiler_params=pltpu.CompilerParams(vmem_limit_bytes=40 * 2**20),
        name="fold",
    )(slots_pair, coeffs)


def legendre_kernel(
    start_ref, a_ref, ab_ref, cos_ref, weight_ref, seed_ref, level_ref, out_ref, rows_ref
):
    x = cos_ref[...]
    weight = weight_ref[...]
    zero = jnp.zeros((8, 128), jnp.float32)

    for j in range(PLANES):
        for h in range(2):
            first = table_base(j) + h * half_rows(j)

            def clear(r, carry, first=first):
                rows_ref[pl.ds(pl.multiple_of(8 * (first + r), 8), 8), :] = zero
                return carry

            lax.fori_loop(0, BLOCK_ROWS, clear, 0, unroll=8)

    tracks = PLANES // 2

    def advance(it, state):
        new_state = []
        for t in range(tracks):
            ja, jb = t, PLANES - 1 - t
            prev, cur, level = state[t]
            ka, kb = start_ref[ja], start_ref[jb]
            first_len = OWNERS - ka
            in_a = it < first_len
            d = jnp.where(in_a, ka + it, kb + it - first_len)
            k = jnp.where(in_a, ka, kb)
            j = jnp.where(in_a, ja, jb)
            fresh = d == k
            prev = jnp.where(fresh, 0.0, prev)
            cur = jnp.where(fresh, seed_ref[j], cur)
            level = jnp.where(fresh, level_ref[j], level)
            biggest = jnp.maximum(jnp.abs(prev), jnp.abs(cur))
            over = biggest > BIG
            factor = jnp.where(over, SHRINK, 1.0)
            prev = prev * factor
            cur = cur * factor
            level = level + jnp.where(over, 1.0, 0.0)
            scale = weight * jnp.exp2(level * STEP_LOG2)
            coef = j * TABLE + STRIDE * d
            per_half = jnp.where(in_a, half_rows(ja), half_rows(jb))
            first = jnp.where(in_a, table_base(ja), table_base(jb)) + 6 * (d - PLANE * j)
            for i in range(STRIDE):
                h, within = divmod(i, 6)
                spot = 8 * (first + h * per_half + within)
                rows_ref[pl.ds(pl.multiple_of(spot, 8), 8), :] = cur * scale
                nxt = (a_ref[coef + i] * x) * cur - ab_ref[coef + i] * prev
                prev, cur = cur, nxt
            new_state.append((prev, cur, level))
        return tuple(new_state)

    lax.fori_loop(0, OWNERS + 1, advance, ((zero, zero, zero),) * tracks)

    def pack(block, carry):
        r0 = pl.multiple_of(block * 16, 16)
        for s in range(8):
            v = rows_ref[pl.ds(8 * r0 + s, 16, stride=8), :]
            out_ref[pl.ds(r0, 16), 128 * s : 128 * (s + 1)] = v.astype(jnp.bfloat16)
        return carry

    lax.fori_loop(0, TABLE_ROWS // 16, pack, 0, unroll=2)


def legendre_tables(start, a_tab, ab_tab, cosine, weight, seed, level):
    smem = pl.BlockSpec(memory_space=pltpu.SMEM)
    vmem = pl.BlockSpec(memory_space=pltpu.VMEM)
    return pl.pallas_call(
        legendre_kernel,
        in_specs=[smem, smem, smem, vmem, vmem, vmem, vmem],
        out_specs=vmem,
        out_shape=jax.ShapeDtypeStruct((TABLE_ROWS, HALF), jnp.bfloat16),
        scratch_shapes=[pltpu.VMEM((8 * TABLE_ROWS, 128), jnp.float32)],
        compiler_params=pltpu.CompilerParams(vmem_limit_bytes=56 * 2**20),
        name="legendre",
    )(start, a_tab, ab_tab, cosine, weight, seed, level)


def transform_kernel(table_hbm, x_ref, out_ref, table, picked, wide, sems):
    copies = []
    for j in range(PLANES):
        for h in range(2):
            first = table_base(j) + h * half_rows(j)
            span = pl.ds(first, half_rows(j))
            copy = pltpu.make_async_copy(table_hbm.at[span], table.at[span], sems.at[2 * j + h])
            copy.start()
            copies.append(copy)
    row = lax.broadcasted_iota(jnp.int32, (512, 512), 0)
    col = lax.broadcasted_iota(jnp.int32, (512, 512), 1)
    source = (row % 32) * 16 + (row // 64) * 2 + (row % 64) // 32
    pick = jnp.where(source == col, 1.0, 0.0).astype(jnp.bfloat16)
    picked[...] = jnp.dot(pick, x_ref[...], preferred_element_type=jnp.float32).astype(jnp.bfloat16)
    contract = (((1,), (1,)), ((), ()))
    for q in range(4):
        mine = picked[128 * q : 128 * (q + 1), :]
        both = jnp.concatenate([mine[:, :HALF], mine[:, HALF:]], axis=0)
        ja, jb = 2 * q, 2 * q + 1
        for h in range(2):
            halves = []
            for j in (ja, jb):
                copies[2 * j + h].wait()
                first = table_base(j) + h * half_rows(j)
                got = lax.dot_general(
                    table[first : first + half_rows(j), :],
                    both,
                    contract,
                    preferred_element_type=jnp.float32,
                )
                parity = lax.broadcasted_iota(jnp.int32, (half_rows(j), 128), 0) % 2
                halves.append(jnp.where(parity == 0, got[:, :128], got[:, 128:]))
            shape = (half_rows(jb), 128)
            lane = lax.broadcasted_iota(jnp.int32, shape, 1)
            joined = jnp.where(lane < 64, halves[0][BLOCK_ROWS:], halves[1])
            lane = lax.broadcasted_iota(jnp.int32, (BLOCK_ROWS, 128), 1)
            opening = jnp.where(lane < 64, halves[0][:BLOCK_ROWS], 0.0)
            base = h * 4 * half_rows(0) + q
            if ja:
                gap = BLOCK_ROWS * ja
                wide[pl.ds(base, gap, stride=4), :] = jnp.zeros((gap, 128), jnp.float32)
            wide[pl.ds(base + 4 * BLOCK_ROWS * ja, BLOCK_ROWS, stride=4), :] = opening
            wide[pl.ds(base + 4 * BLOCK_ROWS * jb, half_rows(jb), stride=4), :] = joined
    out_ref[...] = wide[...].astype(jnp.bfloat16)


def transform(table, x):
    rows = 8 * half_rows(0)
    vmem = pl.BlockSpec(memory_space=pltpu.VMEM)
    return pl.pallas_call(
        transform_kernel,
        in_specs=[pl.BlockSpec(memory_space=pl.ANY), vmem],
        out_specs=vmem,
        out_shape=jax.ShapeDtypeStruct((rows, 128), jnp.bfloat16),
        scratch_shapes=[
            pltpu.VMEM((TABLE_ROWS, HALF), jnp.bfloat16),
            pltpu.VMEM((512, 2 * HALF), jnp.bfloat16),
            pltpu.VMEM((rows, 128), jnp.float32),
            pltpu.SemaphoreType.DMA((16,)),
        ],
        compiler_params=pltpu.CompilerParams(vmem_limit_bytes=56 * 2**20),
        name="transform",
    )(table, x)


def cross_kernel(who_ref, harm_ref, own_ref, other_ref, out_ref, wide):
    i = pl.program_id(0)

    @pl.when(i == 0)
    def _():
        wide[...] = harm_ref[...].astype(jnp.float32)

    tracer, owner = who_ref[0], who_ref[1]
    lane = lax.broadcasted_iota(jnp.int32, (16, 128), 1) // 32
    fields = []
    for t in range(2):
        blocks = []
        for q in range(4):
            tiles = [[], [], [], []]
            for zh in range(2):
                turned = []
                for z4 in range(4):
                    source = (t * OWNERS + (4 * zh + z4) * 16) * 24
                    v = wide[pl.ds(source + 4 * i + q, 16, stride=24), :]
                    turned.append(
                        [v] + [pltpu.roll(v, shift=32 * turn, axis=1) for turn in (1, 2, 3)]
                    )
                for hc in range(4):
                    tile = turned[0][(0 - hc) % 4]
                    for z4 in range(1, 4):
                        tile = jnp.where(lane == z4, turned[z4][(z4 - hc) % 4], tile)
                    tiles[hc].append(tile)
            for hc in range(4):
                blocks.append(jnp.concatenate(tiles[hc], axis=1).astype(jnp.bfloat16))
        fields.append(jnp.concatenate(blocks, axis=0))
    own, other = own_ref[0, 0], other_ref[0]
    first = tracer == 0
    basis_lead = jnp.where(first, own, other)
    basis_trail = jnp.where(first, other, own)
    contract = (((1,), (1,)), ((), ()))
    lead = lax.dot_general(basis_lead, fields[0], contract, preferred_element_type=jnp.float32)
    trail = lax.dot_general(fields[1], basis_trail, contract, preferred_element_type=jnp.float32)
    total = jnp.dot(
        lead.astype(jnp.bfloat16), trail.astype(jnp.bfloat16), preferred_element_type=jnp.float32
    )
    tally = jnp.full((1, 512), owner + 1, jnp.int32).astype(jnp.float32)
    out_ref[0, 0] = total * (1.0 / jnp.sqrt(2.0 * tally))


def cross_spectrum(who, harmonic, bessel, partner):
    return pl.pallas_call(
        cross_kernel,
        grid_spec=pltpu.PrefetchScalarGridSpec(
            num_scalar_prefetch=1,
            grid=(6,),
            in_specs=[
                pl.BlockSpec((256 * 24, 128), lambda i, who: (0, 0)),
                pl.BlockSpec((1, 1, 512, 256), lambda i, who: (0, 6 * who[0] + i, 0, 0)),
                pl.BlockSpec((1, 512, 256), lambda i, who: (i, 0, 0)),
            ],
            out_specs=pl.BlockSpec((1, 1, 512, 512), lambda i, who: (0, i, 0, 0)),
            scratch_shapes=[pltpu.VMEM((256 * 24, 128), jnp.float32)],
        ),
        out_shape=jax.ShapeDtypeStruct((1, 6, 512, 512), jnp.float32),
        compiler_params=pltpu.CompilerParams(vmem_limit_bytes=40 * 2**20),
        name="cross",
    )(who, harmonic, bessel, partner)


def cycle_geometry():
    cycle_number = jnp.arange(1, HALF + 1, dtype=jnp.float32)
    nside_float = jnp.float32(NSIDE)
    polar_cycle = cycle_number < nside_float
    polar_gap = cycle_number * cycle_number / (3.0 * nside_float * nside_float)
    equator_height = 4.0 / 3.0 - 2.0 * cycle_number / (3.0 * nside_float)
    cycle_height = jnp.where(polar_cycle, 1.0 - polar_gap, equator_height)
    height_gap = jnp.where(polar_cycle, polar_gap, 1.0 - equator_height)
    sine_cycle = jnp.sqrt(height_gap * (1.0 + cycle_height))
    pixels = jnp.where(polar_cycle, 4.0 * cycle_number, 4.0 * nside_float)
    weight = jnp.sqrt(jnp.pi * pixels / (3.0 * nside_float * nside_float))
    return (cycle_height, sine_cycle, weight)


def legendre_seed(orders, sine_cycle):
    counter = jnp.arange(1, LMAX + 1, dtype=jnp.float32)
    log_terms = jnp.log1p(-0.5 / counter)
    partial_sum = jnp.sum(
        jnp.where(counter[None, :] <= orders[:, None], log_terms[None, :], 0.0), axis=1
    )
    head = 0.5 * jnp.log((2.0 * orders + 1.0) / (4.0 * jnp.pi)) + 0.5 * partial_sum
    return head[:, None] + orders[:, None] * jnp.log(sine_cycle)[None, :]


def recurrence_tables(orders):
    degree = jnp.arange(1, TABLE + 1, dtype=jnp.float32)[None, :]
    order_col = orders[:, None]
    alpha = jnp.sqrt(
        jnp.maximum(4.0 * degree * degree - 1.0, 1.0)
        / jnp.maximum(degree * degree - order_col * order_col, 1.0)
    )
    below = degree - 1.0
    beta = jnp.sqrt(
        jnp.maximum(below * below - order_col * order_col, 0.0)
        / jnp.maximum(4.0 * below * below - 1.0, 1.0)
    )
    return alpha.reshape(-1), (alpha * beta).reshape(-1)


def per_device(coeffs, bessel, azimuthal_order_slots):
    tracer = lax.axis_index("tracer")
    owner = lax.axis_index("dev")
    place = lax.rem(owner, PLANE)
    plane_groups = [[PLANE * z + i for i in range(PLANE)] for z in range(PLANES)]

    away = lax.dynamic_slice_in_dim(bessel[0], (1 - tracer) * 6, 6, 0)
    partner = lax.ppermute(away, "tracer", [(0, 1), (1, 0)])

    slots_pair = jnp.repeat(azimuthal_order_slots, 2)[None, :]
    folded = fold_coefficients(slots_pair, coeffs[0])
    regrouped = lax.all_to_all(
        folded, "dev", split_axis=0, concat_axis=0, tiled=True, axis_index_groups=plane_groups
    )

    start = order_index(jnp.arange(PLANES, dtype=jnp.int32), place)
    orders = (STRIDE * start).astype(jnp.float32)
    cosine, sine, weight = cycle_geometry()
    seed_log = legendre_seed(orders, sine)
    level = jnp.minimum(jnp.floor(seed_log / (STEP_LN_HIGH + STEP_LN_LOW) + 0.5), 0.0)
    seed = jnp.exp((seed_log - level * STEP_LN_HIGH) - level * STEP_LN_LOW)
    a_tab, ab_tab = recurrence_tables(orders)
    table = legendre_tables(
        start,
        a_tab,
        ab_tab,
        cosine.reshape(8, 128),
        weight.reshape(8, 128),
        seed.reshape(8, 8, 128),
        level.reshape(8, 8, 128),
    )

    harmonic = transform(table, regrouped.reshape(512, 2 * HALF))
    by_degree = lax.all_to_all(
        harmonic.reshape(256, 24, 128), ("tracer", "dev"), split_axis=0, concat_axis=0, tiled=True
    )
    who = jnp.stack([tracer, owner]).astype(jnp.int32)
    return cross_spectrum(who, by_degree.reshape(256 * 24, 128), bessel, partner)


def solution(mesh):
    placed = (P("tracer", "dev", None, None), P("tracer", "dev", None, None), P())
    return jax.shard_map(
        per_device,
        mesh=mesh,
        in_specs=placed,
        out_specs=P("tracer", "dev", None, None),
        check_vma=False,
    )
```

time: 1850 us -> 129 us (0.07)
  loops' own time: 819 us -> 0 us
  blocking collectives: 607 us -> 0 us
  local copies, waits for them, and re-layouts: 203 us -> 10.5 us
  other arithmetic: 97.7 us -> 2.43 us
  Pallas kernels: 0 us -> 51.2 us
  matrix products: 33 us -> 0 us
    another operation x9 -> x0, loops' own time: 819 us -> none  [the longest x8 819 us: legendre_block(): lax.scan(advance, carried, jnp.arange(LB, dtype=jnp.int32), unroll=8)]
    all_to_all x1 -> x0, blocking collectives: 607 us -> none  [per_device(): lax.all_to_all(harmonic.reshape(2 * M_DEV, LMAX, SHELLS), 'dev', split_ax...]
    dynamic_update_slice x136 -> x0, local copies, waits for them, and re-layouts: 89.9 us -> none  [the longest x128 83.5 us: legendre_block(): lax.scan(advance, carried, jnp.arange(LB, dtype=jnp.int32), unroll=8)]
    slice x128 -> x0, local copies, waits for them, and re-layouts: 80 us -> none  [legendre_block(): lax.scan(advance, carried, jnp.arange(LB, dtype=jnp.int32), unroll=8)]
    while x896 -> x0, other arithmetic: 74 us -> none
    pallas_call x0 -> x4, Pallas kernels: none -> 51.2 us  [the longest x1 26.3 us: legendre_tables(): pl.pallas_call(legendre_kernel, in_specs=[smem, smem, smem, vmem, vmem, v...]
    dot_general x10 -> x0, matrix products: 33 us -> none  [the longest x8 21.9 us: fill_block(): jnp.einsum('jhq,vhyq->hyjv', weighted_harmonics, grouped_coefficients, pr...]
    all_to_all x1 -> x2, waiting for transfers between devices: 44.9 us -> 37 us  [the longest x1 35 us: per_device(): lax.all_to_all(harmonic.reshape(256, 24, 128), ('tracer', 'dev'), split_a...]
  transfers between devices with their start and end apart: 2 -> 3, of which waited for: 2 -> 3; matrix products, arithmetic and copies ran while one was open for 0% -> 2% of each run, Pallas kernels for 0% -> 21%
where the time goes in v1:
time: 129 us; the launch traced here: 128 us
  Pallas kernels  51.2 us (40%)
  waiting for transfers between devices  39.9 us (31%)
  starting transfers between devices  24 us (19%)
  local copies, waits for them, and re-layouts  10.5 us (8%)
  other arithmetic  2.43 us (2%)
    all_to_all x1, waiting for transfers between devices, per_device(): lax.all_to_all(harmonic.reshape(256, 24, 128), ('tracer', 'dev'), split_a...  35 us
    pallas_call x1, Pallas kernels, legendre_tables(): pl.pallas_call(legendre_kernel, in_specs=[smem, smem, smem, vmem, vmem, v...  26.3 us
    pallas_call x1, Pallas kernels, transform(): pl.pallas_call(transform_kernel, in_specs=[pl.BlockSpec(memory_space=pl.A...  15.1 us
    all_to_all x1, starting transfers between devices, per_device(): lax.all_to_all(harmonic.reshape(256, 24, 128), ('tracer', 'dev'), split_a...  14.1 us
    unnamed x17, local copies, waits for them, and re-layouts  9.95 us
    pallas_call x1, Pallas kernels, cross_spectrum(): pl.pallas_call(cross_kernel, grid_spec=pltpu.PrefetchScalarGridSpec(num_s...  7.82 us
    all_to_all x1, starting transfers between devices, per_device(): lax.all_to_all(folded, 'dev', split_axis=0, concat_axis=0, tiled=True, ax...  7.57 us
    ppermute x1, waiting for transfers between devices, per_device(): partner = lax.ppermute(away, 'tracer', [(0, 1), (1, 0)])  2.96 us
  transfers between devices with their start and end apart: 3, of which 3 were waited for; matrix products, arithmetic and copies ran while one was open for 2% of the time, Pallas kernels for 21%

profile of v1, /device:TPU:1, one launch (start us, length us, event | category | flops | bytes accessed | tf_op | source)
XLA Modules:
  0.0 128.2 jit_solution(14860362487914249689)
XLA Ops:
  0.0 4.8 %copy.6 = bf16[1,2,256,2047]{3,2,1,0:T(8,128)(2,1)S(1)} copy(bf16[1,2,256,2047]{2,1,3,0:T(2,128)(2,1)} %param.3) | data formatting | bytes 4192256 | tf_op args[0]
  4.8 0.0 copy-done.7
  4.8 0.1 broadcast_in_dim.40
  4.8 0.1 broadcast_in_dim_reshape.3.slots_ref
  5.0 1.9 %fold.1 = bf16[16,2,16,2048]{3,2,1,0:T(8,128)(2,1)S(1)} custom-call(s32[1,256]{1,0:T(1,128)S(1)} %broadcast_in_dim_reshape.3.slots_ref, bf16[2,256,2047]{2,1,0:T(8,128)(2,1)S(1)} %bitcast.8), custom_call_target="tpu_custom_call" | custom-call | tf_op jit(solution)/shard_map/fold/pallas_call | solution.py:74
  6.9 0.0 copy-start
  6.9 1.3 %copy-done = bf16[16,2,16,2048]{3,2,1,0:T(8,128)(2,1)} copy-done((bf16[16,2,16,2048]{3,2,1,0:T(8,128)(2,1)}, bf16[16,2,16,2048]{3,2,1,0:T(8,128)(2,1)S(1)}, u32[]{:S(2)}) %copy-start) | copy-done | bytes 2097176
  8.2 7.6 %all-to-all-start = ((bf16[16,2,16,2048]{3,2,1,0:T(8,128)(2,1)}), bf16[16,2,16,2048]{3,2,1,0:T(8,128)(2,1)S(1)}, u32[]{:S(2)}, u32[]{:S(2)}) async-start(bf16[16,2,16,2048]{3,2,1,0:T(8,128)(2,1)} %copy-done), calls=%async_computation | async-start | bytes 4194304 | tf_op jit(solution)/shard_map/all_to_all | solution.py:346
  15.8 0.0 copy-start.6
  15.9 0.2 select_reduce_fusion
  16.1 0.1 divide_sqrt_fusion
  16.2 0.1 sqrt.21.a_ref
  16.3 0.0 copy-start.5
  16.3 0.1 sqrt.23
  16.4 0.6 mul.170.ab_ref
  17.0 0.6 multiply_sqrt_fusion
  17.7 0.7 floor_minimum_fusion
  18.4 0.0 copy-done.5
  18.4 26.3 %legendre.1.table_hbm = bf16[6912,1024]{1,0:T(8,128)(2,1)} custom-call(s32[8]{0:T(128)} %copy-done.6, f32[12416]{0:T(1024)} %copy-done.5, f32[12416]{0:T(1024)} %mul.170.ab_ref, f32[8,128]{1,0:T(8,128)} %get-tuple-element.20.cos_ref, f32[8,128]{1,0:T(8,128)} %get-tuple-element.19.weight_ref, f32[8,8,128]{2,1,0:T(8,128)} %get-tuple-element.8.seed_ref, ...), custom_call_target="tpu_custom_call" | custom-call | tf_op jit(solution)/shard_map/legendre/pallas_call | solution.py:156
  44.7 2.0 %all-to-all-done = bf16[16,2,16,2048]{3,2,1,0:T(8,128)(2,1)S(1)} async-done(((bf16[16,2,16,2048]{3,2,1,0:T(8,128)(2,1)}), bf16[16,2,16,2048]{3,2,1,0:T(8,128)(2,1)S(1)}, u32[]{:S(2)}, u32[]{:S(2)}) %all-to-all-start) | async-done | bytes 2097184 | tf_op jit(solution)/shard_map/all_to_all | solution.py:346
  46.8 1.3 %copy-done.4 = bf16[16,2,16,2048]{3,2,1,0:T(8,128)(2,1)} copy-done((bf16[16,2,16,2048]{3,2,1,0:T(8,128)(2,1)}, bf16[16,2,16,2048]{3,2,1,0:T(8,128)(2,1)S(1)}, u32[]{:S(2)}) %copy-start.4) | copy-done | bytes 2097176
  48.1 15.1 %transform.1 = bf16[6144,128]{1,0:T(8,128)(2,1)} custom-call(bf16[6912,1024]{1,0:T(8,128)(2,1)} %legendre.1.table_hbm, bf16[512,2048]{1,0:T(8,128)(2,1)} %bitcast.9), custom_call_target="tpu_custom_call" | custom-call | tf_op jit(solution)/shard_map/transform/pallas_call | solution.py:216
  63.2 0.0 copy-start.1
  63.2 14.1 %all-to-all-start.1 = ((bf16[256,24,128]{2,1,0:T(8,128)(2,1)}), bf16[256,24,128]{2,1,0:T(8,128)(2,1)}, u32[]{:S(2)}, u32[]{:S(2)}) async-start(bf16[256,24,128]{2,1,0:T(8,128)(2,1)} %bitcast.10), calls=%async_computation.1 | async-start | bytes 3145728 | tf_op jit(solution)/shard_map/all_to_all | solution.py:368
  77.4 0.1 dynamic-slice_bitcast_fusion
  77.5 2.3 %collective-permute-start = (bf16[6,512,256]{2,1,0:T(8,128)(2,1)S(1)}, bf16[6,512,256]{2,1,0:T(8,128)(2,1)S(1)}, u32[]{:S(2)}, u32[]{:S(2)}) collective-permute-start(bf16[6,512,256]{2,1,0:T(8,128)(2,1)S(1)} %dynamic-slice_bitcast_fusion), channel_id=1, source_target_pairs={{0,128},{128,0},{1,129},{129,1},{2,130},{130,2},{3,131},{131,3},{4... | collective-permute-start | bytes 4718600 | tf_op jit(solution)/shard_map/ppermute | solution.py:342
  79.8 0.1 pad_add_fusion.who_ref
  79.9 3.0 %collective-permute-done.other_ref = bf16[6,512,256]{2,1,0:T(8,128)(2,1)S(1)} collective-permute-done((bf16[6,512,256]{2,1,0:T(8,128)(2,1)S(1)}, bf16[6,512,256]{2,1,0:T(8,128)(2,1)S(1)}, u32[]{:S(2)}, u32[]{:S(2)}) %collective-permute-start) | collective-permute-done | bytes 1572896 | tf_op jit(solution)/shard_map/ppermute | solution.py:342
  82.8 1.1 copy-done.2
  84.0 35.0 %all-to-all-done.1 = bf16[256,24,128]{2,1,0:T(8,128)(2,1)} async-done(((bf16[256,24,128]{2,1,0:T(8,128)(2,1)}), bf16[256,24,128]{2,1,0:T(8,128)(2,1)}, u32[]{:S(2)}, u32[]{:S(2)}) %all-to-all-start.1) | async-done | bytes 1572896 | tf_op jit(solution)/shard_map/all_to_all | solution.py:368
  118.9 1.4 %copy-done.3 = bf16[6,512,256]{2,1,0:T(8,128)(2,1)S(1)} copy-done((bf16[6,512,256]{2,1,0:T(8,128)(2,1)S(1)}, bf16[6,512,256]{2,1,0:T(8,128)(2,1)}, u32[]{:S(2)}) %copy-start.3) | copy-done | bytes 1572888
  120.3 7.8 %cross.1 = f32[1,6,512,512]{3,2,1,0:T(8,128)} custom-call(s32[2]{0:T(128)S(1)} %pad_add_fusion.who_ref, bf16[6144,128]{1,0:T(8,128)(2,1)} %bitcast.5.harm_ref, bf16[1,12,512,256]{3,2,1,0:T(8,128)(2,1)S(1)} %copy-done.1, bf16[6,512,256]{2,1,0:T(8,128)(2,1)S(1)} %copy-done.3), custom_call_target="tpu_custom_call" | custom-call | tf_op jit(solution)/shard_map/cross/pallas_call | solution.py:277
  (12 shorter events, 0.1 us)
Async XLA Ops:
  0.0 4.8 %copy-start.7 = (s32[128]{0:T(128)S(1)}, s32[128]{0:T(128)}, u32[]{:S(2)}) copy-start(s32[128]{0:T(128)} %param.5) | copy-start | bytes 1540
  6.9 1.3 %copy-start = (bf16[16,2,16,2048]{3,2,1,0:T(8,128)(2,1)}, bf16[16,2,16,2048]{3,2,1,0:T(8,128)(2,1)S(1)}, u32[]{:S(2)}) copy-start(bf16[16,2,16,2048]{3,2,1,0:T(8,128)(2,1)S(1)} %fold.1) | copy-start | bytes 6291460
  8.2 38.5 %all-to-all-start = ((bf16[16,2,16,2048]{3,2,1,0:T(8,128)(2,1)}), bf16[16,2,16,2048]{3,2,1,0:T(8,128)(2,1)S(1)}, u32[]{:S(2)}, u32[]{:S(2)}) async-start(bf16[16,2,16,2048]{3,2,1,0:T(8,128)(2,1)} %copy-done), calls=%async_computation | async-start | bytes 4194304 | tf_op jit(solution)/shard_map/all_to_all | solution.py:346
  15.8 2.6 %copy-start.6 = (s32[8]{0:T(128)}, s32[8]{0:T(128)S(1)}, u32[]{:S(2)}) copy-start(s32[8]{0:T(128)S(1)} %get-tuple-element.6.start_ref) | copy-start | bytes 100
  16.3 2.1 %copy-start.5 = (f32[12416]{0:T(1024)}, f32[12416]{0:T(1024)S(1)}, u32[]{:S(2)}) copy-start(f32[12416]{0:T(1024)S(1)} %sqrt.21.a_ref) | copy-start | bytes 148996
  46.7 1.3 %copy-start.4 = (bf16[16,2,16,2048]{3,2,1,0:T(8,128)(2,1)}, bf16[16,2,16,2048]{3,2,1,0:T(8,128)(2,1)S(1)}, u32[]{:S(2)}) copy-start(bf16[16,2,16,2048]{3,2,1,0:T(8,128)(2,1)S(1)} %all-to-all-done) | copy-start | bytes 6291460
  63.2 14.2 %copy-start.1 = (bf16[1,12,512,256]{3,2,1,0:T(8,128)(2,1)S(1)}, bf16[1,12,512,256]{3,2,1,0:T(8,128)(2,1)}, u32[]{:S(2)}) copy-start(bf16[1,12,512,256]{3,2,1,0:T(8,128)(2,1)} %own_ref.1) | copy-start | bytes 9437188
  63.2 55.7 %all-to-all-start.1 = ((bf16[256,24,128]{2,1,0:T(8,128)(2,1)}), bf16[256,24,128]{2,1,0:T(8,128)(2,1)}, u32[]{:S(2)}, u32[]{:S(2)}) async-start(bf16[256,24,128]{2,1,0:T(8,128)(2,1)} %bitcast.10), calls=%async_computation.1 | async-start | bytes 3145728 | tf_op jit(solution)/shard_map/all_to_all | solution.py:368
  77.5 5.3 %collective-permute-start = (bf16[6,512,256]{2,1,0:T(8,128)(2,1)S(1)}, bf16[6,512,256]{2,1,0:T(8,128)(2,1)S(1)}, u32[]{:S(2)}, u32[]{:S(2)}) collective-permute-start(bf16[6,512,256]{2,1,0:T(8,128)(2,1)S(1)} %dynamic-slice_bitcast_fusion), channel_id=1, source_target_pairs={{0,128},{128,0},{1,129},{129,1},{2,130},{130,2},{3,131},{131,3},{4... | collective-permute-start | bytes 4718600 | tf_op jit(solution)/shard_map/ppermute | solution.py:342
  82.8 1.1 copy-start.2
  118.9 1.4 %copy-start.3 = (bf16[6,512,256]{2,1,0:T(8,128)(2,1)S(1)}, bf16[6,512,256]{2,1,0:T(8,128)(2,1)}, u32[]{:S(2)}) copy-start(bf16[6,512,256]{2,1,0:T(8,128)(2,1)} %copy-done.2) | copy-start | bytes 4718596

commit v2 on v1

--- a/solution.py
+++ b/solution.py
@@ -14,7 +14,9 @@
 PLANES = 8
 OWNERS = 128
 TABLE = LMAX + 16
-BLOCK_ROWS = 6 * PLANE
+CHAINS = 4
+SPREAD = OWNERS // CHAINS
+BLOCK_ROWS = 6 * SPREAD
 STEP_LOG2 = 64.0
 STEP_LN_HIGH = 44.359375
 STEP_LN_LOW = 0.0020445558364884
@@ -23,29 +25,29 @@
 
 
 def half_rows(j):
-    return BLOCK_ROWS * (PLANES - j)
+    return BLOCK_ROWS * (CHAINS - j)
 
 
 def table_base(j):
     return sum(2 * half_rows(i) for i in range(j))
 
 
-TABLE_ROWS = table_base(PLANES)
+TABLE_ROWS = table_base(CHAINS)
 
 
 def order_index(j, place):
     flip = lax.rem(j, 2)
-    return PLANE * j + jnp.where(flip == 0, place, PLANE - 1 - place)
+    return SPREAD * j + jnp.where(flip == 0, place, SPREAD - 1 - place)
 
 
 def fold_kernel(slots_ref, coef_ref, out_ref):
     x = coef_ref[0]
     row = lax.broadcasted_iota(jnp.int32, (256, 256), 0)
     col = lax.broadcasted_iota(jnp.int32, (256, 256), 1)
-    group = row // 16
-    j = (row % 16) // 2
-    place = jnp.where(j % 2 == 0, group, PLANE - 1 - group)
-    wanted = STRIDE * (PLANE * j + place)
+    member = row // 8
+    j = (row % 8) // 2
+    place = jnp.where(j % 2 == 0, member, SPREAD - 1 - member)
+    wanted = STRIDE * (SPREAD * j + place)
     hit = jnp.logical_and(slots_ref[...] == wanted, row % 2 == col % 2)
     pick = jnp.where(hit, 1.0, 0.0).astype(jnp.bfloat16)
     south = x[:, HALF:].astype(jnp.float32)
@@ -66,8 +68,8 @@
         here = north[:, 128 * b : 128 * (b + 1)]
         even = (here + mirrored).astype(jnp.bfloat16)
         odd = (here - mirrored).astype(jnp.bfloat16)
-        out_ref[:, 0, :, 128 * b : 128 * (b + 1)] = even.reshape(16, 16, 128)
-        out_ref[:, 0, :, HALF + 128 * b : HALF + 128 * (b + 1)] = odd.reshape(16, 16, 128)
+        out_ref[:, 0, :, 128 * b : 128 * (b + 1)] = even.reshape(32, 8, 128)
+        out_ref[:, 0, :, HALF + 128 * b : HALF + 128 * (b + 1)] = odd.reshape(32, 8, 128)
 
 
 def fold_coefficients(slots_pair, coeffs):
@@ -78,9 +80,9 @@
             pl.BlockSpec((1, 256), lambda s: (0, 0)),
             pl.BlockSpec((1, 256, 2 * HALF), lambda s: (s, 0, 0)),
         ],
-        out_specs=pl.BlockSpec((16, 1, 16, 2 * HALF), lambda s: (0, s, 0, 0)),
-        out_shape=jax.ShapeDtypeStruct((16, 2, 16, 2 * HALF), jnp.bfloat16),
-        compiler_params=pltpu.CompilerParams(vmem_limit_bytes=40 * 2**20),
+        out_specs=pl.BlockSpec((32, 1, 8, 2 * HALF), lambda s: (0, s, 0, 0)),
+        out_shape=jax.ShapeDtypeStruct((32, 2, 8, 2 * HALF), jnp.bfloat16),
+        compiler_params=pltpu.CompilerParams(vmem_limit_bytes=58 * 2**20),
         name="fold",
     )(slots_pair, coeffs)
 
@@ -92,7 +94,7 @@
     weight = weight_ref[...]
     zero = jnp.zeros((8, 128), jnp.float32)
 
-    for j in range(PLANES):
+    for j in range(CHAINS):
         for h in range(2):
             first = table_base(j) + h * half_rows(j)
 
@@ -102,12 +104,12 @@
 
             lax.fori_loop(0, BLOCK_ROWS, clear, 0, unroll=8)
 
-    tracks = PLANES // 2
+    tracks = CHAINS // 2
 
     def advance(it, state):
         new_state = []
         for t in range(tracks):
-            ja, jb = t, PLANES - 1 - t
+            ja, jb = t, CHAINS - 1 - t
             prev, cur, level = state[t]
             ka, kb = start_ref[ja], start_ref[jb]
             first_len = OWNERS - ka
@@ -128,7 +130,7 @@
             scale = weight * jnp.exp2(level * STEP_LOG2)
             coef = j * TABLE + STRIDE * d
             per_half = jnp.where(in_a, half_rows(ja), half_rows(jb))
-            first = jnp.where(in_a, table_base(ja), table_base(jb)) + 6 * (d - PLANE * j)
+            first = jnp.where(in_a, table_base(ja), table_base(jb)) + 6 * (d - SPREAD * j)
             for i in range(STRIDE):
                 h, within = divmod(i, 6)
                 spot = 8 * (first + h * per_half + within)
@@ -144,7 +146,7 @@
         r0 = pl.multiple_of(block * 16, 16)
         for s in range(8):
             v = rows_ref[pl.ds(8 * r0 + s, 16, stride=8), :]
-            out_ref[pl.ds(r0, 16), 128 * s : 128 * (s + 1)] = v.astype(jnp.bfloat16)
+            out_ref[s, pl.ds(r0, 16), :] = v.astype(jnp.bfloat16)
         return carry
 
     lax.fori_loop(0, TABLE_ROWS // 16, pack, 0, unroll=2)
@@ -157,57 +159,60 @@
         legendre_kernel,
         in_specs=[smem, smem, smem, vmem, vmem, vmem, vmem],
         out_specs=vmem,
-        out_shape=jax.ShapeDtypeStruct((TABLE_ROWS, HALF), jnp.bfloat16),
+        out_shape=jax.ShapeDtypeStruct((8, TABLE_ROWS, 128), jnp.bfloat16),
         scratch_shapes=[pltpu.VMEM((8 * TABLE_ROWS, 128), jnp.float32)],
         compiler_params=pltpu.CompilerParams(vmem_limit_bytes=56 * 2**20),
         name="legendre",
     )(start, a_tab, ab_tab, cosine, weight, seed, level)
 
 
-def transform_kernel(table_hbm, x_ref, out_ref, table, picked, wide, sems):
+def transform_kernel(table_hbm, x_ref, out_hbm, table, picked, wide, packed, sems):
     copies = []
-    for j in range(PLANES):
-        for h in range(2):
-            first = table_base(j) + h * half_rows(j)
-            span = pl.ds(first, half_rows(j))
-            copy = pltpu.make_async_copy(table_hbm.at[span], table.at[span], sems.at[2 * j + h])
+    for h in range(2):
+        for j in range(CHAINS):
+            span = pl.ds(table_base(j) + h * half_rows(j), half_rows(j))
+            copy = pltpu.make_async_copy(
+                table_hbm.at[:, span], table.at[:, span], sems.at[CHAINS * h + j]
+            )
             copy.start()
             copies.append(copy)
-    row = lax.broadcasted_iota(jnp.int32, (512, 512), 0)
-    col = lax.broadcasted_iota(jnp.int32, (512, 512), 1)
-    source = (row % 32) * 16 + (row // 64) * 2 + (row % 64) // 32
+    row = lax.broadcasted_iota(jnp.int32, (256, 256), 0)
+    col = lax.broadcasted_iota(jnp.int32, (256, 256), 1)
+    shell = row % 32
+    source = (shell // 2) * 16 + (shell % 2) * 8 + (row // 64) * 2 + (row % 64) // 32
     pick = jnp.where(source == col, 1.0, 0.0).astype(jnp.bfloat16)
-    picked[...] = jnp.dot(pick, x_ref[...], preferred_element_type=jnp.float32).astype(jnp.bfloat16)
+    for t in range(2):
+        got = jnp.dot(
+            pick, x_ref[256 * t : 256 * (t + 1), :], preferred_element_type=jnp.float32
+        ).astype(jnp.bfloat16)
+        for j in range(CHAINS):
+            mine = got[64 * j : 64 * (j + 1)]
+            picked[j, 64 * t : 64 * (t + 1), :] = mine[:, :HALF]
+            picked[j, 128 + 64 * t : 128 + 64 * (t + 1), :] = mine[:, HALF:]
     contract = (((1,), (1,)), ((), ()))
-    for q in range(4):
-        mine = picked[128 * q : 128 * (q + 1), :]
-        both = jnp.concatenate([mine[:, :HALF], mine[:, HALF:]], axis=0)
-        ja, jb = 2 * q, 2 * q + 1
-        for h in range(2):
-            halves = []
-            for j in (ja, jb):
-                copies[2 * j + h].wait()
-                first = table_base(j) + h * half_rows(j)
-                got = lax.dot_general(
-                    table[first : first + half_rows(j), :],
-                    both,
-                    contract,
-                    preferred_element_type=jnp.float32,
-                )
-                parity = lax.broadcasted_iota(jnp.int32, (half_rows(j), 128), 0) % 2
-                halves.append(jnp.where(parity == 0, got[:, :128], got[:, 128:]))
-            shape = (half_rows(jb), 128)
-            lane = lax.broadcasted_iota(jnp.int32, shape, 1)
-            joined = jnp.where(lane < 64, halves[0][BLOCK_ROWS:], halves[1])
-            lane = lax.broadcasted_iota(jnp.int32, (BLOCK_ROWS, 128), 1)
-            opening = jnp.where(lane < 64, halves[0][:BLOCK_ROWS], 0.0)
-            base = h * 4 * half_rows(0) + q
-            if ja:
-                gap = BLOCK_ROWS * ja
+    for h in range(2):
+        for j in range(CHAINS):
+            both = picked[j]
+            copies[CHAINS * h + j].wait()
+            first = table_base(j) + h * half_rows(j)
+            last = first + half_rows(j)
+            rows = jnp.concatenate([table[s, first:last, :] for s in range(8)], axis=1)
+            got = lax.dot_general(rows, both, contract, preferred_element_type=jnp.float32)
+            parity = lax.broadcasted_iota(jnp.int32, (half_rows(j), 128), 0) % 2
+            base = h * 4 * half_rows(0) + j
+            gap = BLOCK_ROWS * j
+            if gap:
                 wide[pl.ds(base, gap, stride=4), :] = jnp.zeros((gap, 128), jnp.float32)
-            wide[pl.ds(base + 4 * BLOCK_ROWS * ja, BLOCK_ROWS, stride=4), :] = opening
-            wide[pl.ds(base + 4 * BLOCK_ROWS * jb, half_rows(jb), stride=4), :] = joined
-    out_ref[...] = wide[...].astype(jnp.bfloat16)
+            wide[pl.ds(base + 4 * gap, half_rows(j), stride=4), :] = jnp.where(
+                parity == 0, got[:, :128], got[:, 128:]
+            )
+        half = pl.ds(h * 4 * half_rows(0), 4 * half_rows(0))
+        packed[half, :] = wide[half, :].astype(jnp.bfloat16)
+        copy = pltpu.make_async_copy(packed.at[half], out_hbm.at[half], sems.at[2 * CHAINS + h])
+        copy.start()
+        copies.append(copy)
+    for copy in copies[2 * CHAINS :]:
+        copy.wait()
 
 
 def transform(table, x):
@@ -216,15 +221,16 @@
     return pl.pallas_call(
         transform_kernel,
         in_specs=[pl.BlockSpec(memory_space=pl.ANY), vmem],
-        out_specs=vmem,
+        out_specs=pl.BlockSpec(memory_space=pltpu.HBM),
         out_shape=jax.ShapeDtypeStruct((rows, 128), jnp.bfloat16),
         scratch_shapes=[
-            pltpu.VMEM((TABLE_ROWS, HALF), jnp.bfloat16),
-            pltpu.VMEM((512, 2 * HALF), jnp.bfloat16),
+            pltpu.VMEM((8, TABLE_ROWS, 128), jnp.bfloat16),
+            pltpu.VMEM((CHAINS, 256, HALF), jnp.bfloat16),
             pltpu.VMEM((rows, 128), jnp.float32),
-            pltpu.SemaphoreType.DMA((16,)),
+            pltpu.VMEM((rows, 128), jnp.bfloat16),
+            pltpu.SemaphoreType.DMA((2 * CHAINS + 2,)),
         ],
-        compiler_params=pltpu.CompilerParams(vmem_limit_bytes=56 * 2**20),
+        compiler_params=pltpu.CompilerParams(vmem_limit_bytes=54 * 2**20),
         name="transform",
     )(table, x)
 
@@ -238,27 +244,28 @@
 
     tracer, owner = who_ref[0], who_ref[1]
     lane = lax.broadcasted_iota(jnp.int32, (16, 128), 1) // 32
-    fields = []
-    for t in range(2):
-        blocks = []
-        for q in range(4):
+    blocks = [[], []]
+    for core in range(2):
+        for j in range(CHAINS):
             tiles = [[], [], [], []]
             for zh in range(2):
                 turned = []
                 for z4 in range(4):
-                    source = (t * OWNERS + (4 * zh + z4) * 16) * 24
-                    v = wide[pl.ds(source + 4 * i + q, 16, stride=24), :]
+                    source = (core * OWNERS + (4 * zh + z4) * PLANE) * 24
+                    v = wide[pl.ds(source + 4 * i + j, PLANE, stride=24), :]
                     turned.append(
                         [v] + [pltpu.roll(v, shift=32 * turn, axis=1) for turn in (1, 2, 3)]
                     )
-                for hc in range(4):
-                    tile = turned[0][(0 - hc) % 4]
+                for part in range(4):
+                    tile = turned[0][(0 - part) % 4]
                     for z4 in range(1, 4):
-                        tile = jnp.where(lane == z4, turned[z4][(z4 - hc) % 4], tile)
-                    tiles[hc].append(tile)
-            for hc in range(4):
-                blocks.append(jnp.concatenate(tiles[hc], axis=1).astype(jnp.bfloat16))
-        fields.append(jnp.concatenate(blocks, axis=0))
+                        tile = jnp.where(lane == z4, turned[z4][(z4 - part) % 4], tile)
+                    tiles[part].append(tile)
+            for part in range(4):
+                blocks[part // 2].append(
+                    jnp.concatenate(tiles[part], axis=1).astype(jnp.bfloat16)
+                )
+    fields = [jnp.concatenate(rows, axis=0) for rows in blocks]
     own, other = own_ref[0, 0], other_ref[0]
     first = tracer == 0
     basis_lead = jnp.where(first, own, other)
@@ -288,7 +295,7 @@
             scratch_shapes=[pltpu.VMEM((256 * 24, 128), jnp.float32)],
         ),
         out_shape=jax.ShapeDtypeStruct((1, 6, 512, 512), jnp.float32),
-        compiler_params=pltpu.CompilerParams(vmem_limit_bytes=40 * 2**20),
+        compiler_params=pltpu.CompilerParams(vmem_limit_bytes=50 * 2**20),
         name="cross",
     )(who, harmonic, bessel, partner)
 
@@ -335,8 +342,10 @@
 def per_device(coeffs, bessel, azimuthal_order_slots):
     tracer = lax.axis_index("tracer")
     owner = lax.axis_index("dev")
-    place = lax.rem(owner, PLANE)
-    plane_groups = [[PLANE * z + i for i in range(PLANE)] for z in range(PLANES)]
+    place = PLANE * tracer + lax.rem(owner, PLANE)
+    plane_groups = [
+        [OWNERS * t + PLANE * z + i for t in range(2) for i in range(PLANE)] for z in range(PLANES)
+    ]
 
     away = lax.dynamic_slice_in_dim(bessel[0], (1 - tracer) * 6, 6, 0)
     partner = lax.ppermute(away, "tracer", [(0, 1), (1, 0)])
@@ -344,10 +353,15 @@
     slots_pair = jnp.repeat(azimuthal_order_slots, 2)[None, :]
     folded = fold_coefficients(slots_pair, coeffs[0])
     regrouped = lax.all_to_all(
-        folded, "dev", split_axis=0, concat_axis=0, tiled=True, axis_index_groups=plane_groups
-    )
-
-    start = order_index(jnp.arange(PLANES, dtype=jnp.int32), place)
+        folded,
+        ("tracer", "dev"),
+        split_axis=0,
+        concat_axis=0,
+        tiled=True,
+        axis_index_groups=plane_groups,
+    )
+
+    start = order_index(jnp.arange(CHAINS, dtype=jnp.int32), place)
     orders = (STRIDE * start).astype(jnp.float32)
     cosine, sine, weight = cycle_geometry()
     seed_log = legendre_seed(orders, sine)
@@ -360,8 +374,8 @@
         ab_tab,
         cosine.reshape(8, 128),
         weight.reshape(8, 128),
-        seed.reshape(8, 8, 128),
-        level.reshape(8, 8, 128),
+        seed.reshape(CHAINS, 8, 128),
+        level.reshape(CHAINS, 8, 128),
     )
 
     harmonic = transform(table, regrouped.reshape(512, 2 * HALF))

time: 129 us -> 122 us (0.946)
  Pallas kernels: 51.2 us -> 37.4 us
  waiting for transfers between devices: 39.9 us -> 48.8 us
  starting transfers between devices: 24 us -> 22.4 us
    pallas_call x1, Pallas kernels: 26.3 us -> 15.5 us  [legendre_tables(): pl.pallas_call(legendre_kernel, in_specs=[smem, smem, smem, vmem, vmem, v...]
    all_to_all x1, waiting for transfers between devices: 2.02 us -> 10.3 us  [per_device(): lax.all_to_all(folded, ('tracer', 'dev'), split_axis=0, concat_axis=0, ti...]
    pallas_call x1, Pallas kernels: 15.1 us -> 9.82 us  [transform(): pl.pallas_call(transform_kernel, in_specs=[pl.BlockSpec(memory_space=pl.A...]
    all_to_all x1, starting transfers between devices: 14.1 us -> 11.6 us  [per_device(): lax.all_to_all(harmonic.reshape(256, 24, 128), ('tracer', 'dev'), split_a...]
    unnamed x17 -> x9, local copies, waits for them, and re-layouts: 9.95 us -> 7.48 us
    pallas_call x1, Pallas kernels: 1.88 us -> 4.09 us  [fold_coefficients(): pl.pallas_call(fold_kernel, grid=(2,), in_specs=[pl.BlockSpec((1, 256), l...]
    dynamic_slice x1, local copies, waits for them, and re-layouts: 0.11 us -> 1.51 us  [per_device(): away = lax.dynamic_slice_in_dim(bessel[0], (1 - tracer) * 6, 6, 0)]
  transfers between devices with their start and end apart: 3 -> 3, of which waited for: 3 -> 3; matrix products, arithmetic and copies ran while one was open for 2% -> 3% of each run, Pallas kernels for 21% -> 13%
where the time goes in v2:
time: 122 us; the launch traced here: 121 us
  waiting for transfers between devices  48.8 us (40%)
  Pallas kernels  37.4 us (31%)
  starting transfers between devices  22.4 us (18%)
  local copies, waits for them, and re-layouts  9.94 us (8%)
  other arithmetic  2.39 us (2%)
    all_to_all x1, waiting for transfers between devices, per_device(): lax.all_to_all(harmonic.reshape(256, 24, 128), ('tracer', 'dev'), split_a...  35.5 us
    pallas_call x1, Pallas kernels, legendre_tables(): pl.pallas_call(legendre_kernel, in_specs=[smem, smem, smem, vmem, vmem, v...  15.5 us
    all_to_all x1, starting transfers between devices, per_device(): lax.all_to_all(harmonic.reshape(256, 24, 128), ('tracer', 'dev'), split_a...  11.6 us
    all_to_all x1, waiting for transfers between devices, per_device(): lax.all_to_all(folded, ('tracer', 'dev'), split_axis=0, concat_axis=0, ti...  10.3 us
    pallas_call x1, Pallas kernels, transform(): pl.pallas_call(transform_kernel, in_specs=[pl.BlockSpec(memory_space=pl.A...  9.82 us
    all_to_all x1, starting transfers between devices, per_device(): lax.all_to_all(folded, ('tracer', 'dev'), split_axis=0, concat_axis=0, ti...  8.59 us
    pallas_call x1, Pallas kernels, cross_spectrum(): pl.pallas_call(cross_kernel, grid_spec=pltpu.PrefetchScalarGridSpec(num_s...  8.01 us
    unnamed x9, local copies, waits for them, and re-layouts  7.48 us
  transfers between devices with their start and end apart: 3, of which 3 were waited for; matrix products, arithmetic and copies ran while one was open for 3% of the time, Pallas kernels for 13%

profile of v2, /device:TPU:1, one launch (start us, length us, event | category | flops | bytes accessed | tf_op | source)
XLA Modules:
  0.0 121.0 jit_solution(13343966972183553754)
XLA Ops:
  0.0 0.0 copy-start.3
  0.0 6.1 %copy.6 = bf16[1,2,256,2047]{3,2,1,0:T(8,128)(2,1)} copy(bf16[1,2,256,2047]{2,1,3,0:T(2,128)(2,1)} %param.3) | data formatting | bytes 4192256 | tf_op args[0]
  6.2 0.0 copy-done.3
  6.2 0.1 broadcast_in_dim.40
  6.2 0.7 broadcast_in_dim_reshape.3.slots_ref
  6.9 4.1 %fold.1 = bf16[32,2,8,2048]{3,2,1,0:T(8,128)(2,1)} custom-call(s32[1,256]{1,0:T(1,128)} %broadcast_in_dim_reshape.3.slots_ref, bf16[2,256,2047]{2,1,0:T(8,128)(2,1)} %bitcast.9), custom_call_target="tpu_custom_call" | custom-call | tf_op jit(solution)/shard_map/fold/pallas_call | solution.py:76
  11.0 8.6 %all-to-all-start = ((bf16[32,2,8,2048]{3,2,1,0:T(8,128)(2,1)}), bf16[32,2,8,2048]{3,2,1,0:T(8,128)(2,1)S(1)}, u32[]{:S(2)}, u32[]{:S(2)}) async-start(bf16[32,2,8,2048]{3,2,1,0:T(8,128)(2,1)} %fold.1), calls=%async_computation | async-start | bytes 4194304 | tf_op jit(solution)/shard_map/all_to_all | solution.py:355
  19.6 0.0 copy-start.2
  19.7 0.2 select_reduce_fusion
  19.9 0.1 divide_sqrt_fusion
  20.0 0.1 sqrt.21.a_ref
  20.1 0.0 copy-start.1
  20.1 0.1 sqrt.23
  20.2 0.6 mul.174.ab_ref
  20.9 0.6 multiply_sqrt_fusion
  21.5 0.7 floor_minimum_fusion
  22.2 0.0 copy-done.2
  22.2 0.0 copy-done.1
  22.2 15.5 %legendre.1.table_hbm = bf16[8,3840,128]{2,1,0:T(8,128)(2,1)} custom-call(s32[4]{0:T(128)} %copy-done.2, f32[6208]{0:T(1024)} %copy-done.1, f32[6208]{0:T(1024)} %mul.174.ab_ref, f32[8,128]{1,0:T(8,128)} %get-tuple-element.20.cos_ref, f32[8,128]{1,0:T(8,128)} %get-tuple-element.19.weight_ref, f32[4,8,128]{2,1,0:T(8,128)} %get-tuple-element.8.seed_ref, ...), custom_call_target="tpu_custom_call" | custom-call | tf_op jit(solution)/shard_map/legendre/pallas_call | solution.py:158
  37.6 10.3 %all-to-all-done = bf16[32,2,8,2048]{3,2,1,0:T(8,128)(2,1)S(1)} async-done(((bf16[32,2,8,2048]{3,2,1,0:T(8,128)(2,1)}), bf16[32,2,8,2048]{3,2,1,0:T(8,128)(2,1)S(1)}, u32[]{:S(2)}, u32[]{:S(2)}) %all-to-all-start) | async-done | bytes 2097184 | tf_op jit(solution)/shard_map/all_to_all | solution.py:355
  47.9 0.0 copy-start
  47.9 1.3 %copy-done = bf16[32,2,8,2048]{3,2,1,0:T(8,128)(2,1)} copy-done((bf16[32,2,8,2048]{3,2,1,0:T(8,128)(2,1)}, bf16[32,2,8,2048]{3,2,1,0:T(8,128)(2,1)S(1)}, u32[]{:S(2)}) %copy-start) | copy-done | bytes 2097176
  49.2 9.8 %transform.1 = bf16[6144,128]{1,0:T(8,128)(2,1)} custom-call(bf16[8,3840,128]{2,1,0:T(8,128)(2,1)} %legendre.1.table_hbm, bf16[512,2048]{1,0:T(8,128)(2,1)} %bitcast.10), custom_call_target="tpu_custom_call" | custom-call | tf_op jit(solution)/shard_map/transform/pallas_call | solution.py:221
  59.1 11.6 %all-to-all-start.1 = ((bf16[256,24,128]{2,1,0:T(8,128)(2,1)}), bf16[256,24,128]{2,1,0:T(8,128)(2,1)S(1)}, u32[]{:S(2)}, u32[]{:S(2)}) async-start(bf16[256,24,128]{2,1,0:T(8,128)(2,1)} %bitcast.11), calls=%async_computation.1 | async-start | bytes 3145728 | tf_op jit(solution)/shard_map/all_to_all | solution.py:382
  70.6 1.5 %dynamic-slice_bitcast_fusion = bf16[6,512,256]{2,1,0:T(8,128)(2,1)S(1)} fusion(bf16[1,12,512,256]{3,2,1,0:T(8,128)(2,1)} %own_ref.1, s32[]{:T(128)S(6)} %select_n.49), kind=kLoop, calls=%fused_computation | loop fusion | bytes 3145732 | tf_op jit(solution)/shard_map/dynamic_slice | solution.py:350
  72.2 2.2 %collective-permute-start = (bf16[6,512,256]{2,1,0:T(8,128)(2,1)S(1)}, bf16[6,512,256]{2,1,0:T(8,128)(2,1)S(1)}, u32[]{:S(2)}, u32[]{:S(2)}) collective-permute-start(bf16[6,512,256]{2,1,0:T(8,128)(2,1)S(1)} %dynamic-slice_bitcast_fusion), channel_id=1, source_target_pairs={{0,128},{128,0},{1,129},{129,1},{2,130},{130,2},{3,131},{131,3},{4... | collective-permute-start | bytes 4718600 | tf_op jit(solution)/shard_map/ppermute | solution.py:351
  74.4 0.1 pad_add_fusion.who_ref
  74.5 3.0 %collective-permute-done.other_ref = bf16[6,512,256]{2,1,0:T(8,128)(2,1)S(1)} collective-permute-done((bf16[6,512,256]{2,1,0:T(8,128)(2,1)S(1)}, bf16[6,512,256]{2,1,0:T(8,128)(2,1)S(1)}, u32[]{:S(2)}, u32[]{:S(2)}) %collective-permute-start) | collective-permute-done | bytes 1572896 | tf_op jit(solution)/shard_map/ppermute | solution.py:351
  77.4 35.5 %all-to-all-done.1 = bf16[256,24,128]{2,1,0:T(8,128)(2,1)S(1)} async-done(((bf16[256,24,128]{2,1,0:T(8,128)(2,1)}), bf16[256,24,128]{2,1,0:T(8,128)(2,1)S(1)}, u32[]{:S(2)}, u32[]{:S(2)}) %all-to-all-start.1) | async-done | bytes 1572896 | tf_op jit(solution)/shard_map/all_to_all | solution.py:382
  113.0 8.0 %cross.1 = f32[1,6,512,512]{3,2,1,0:T(8,128)} custom-call(s32[2]{0:T(128)S(1)} %pad_add_fusion.who_ref, bf16[6144,128]{1,0:T(8,128)(2,1)S(1)} %bitcast.8, bf16[1,12,512,256]{3,2,1,0:T(8,128)(2,1)} %own_ref.1, bf16[6,512,256]{2,1,0:T(8,128)(2,1)S(1)} %collective-permute-done.other_ref), custom_call_target="tpu_custom_call" | custom-call | tf_op jit(solution)/shard_map/cross/pallas_call | solution.py:284
  (6 shorter events, 0.1 us)
Async XLA Ops:
  0.0 6.2 %copy-start.3 = (s32[128]{0:T(128)S(1)}, s32[128]{0:T(128)}, u32[]{:S(2)}) copy-start(s32[128]{0:T(128)} %param.5) | copy-start | bytes 1540
  11.0 36.9 %all-to-all-start = ((bf16[32,2,8,2048]{3,2,1,0:T(8,128)(2,1)}), bf16[32,2,8,2048]{3,2,1,0:T(8,128)(2,1)S(1)}, u32[]{:S(2)}, u32[]{:S(2)}) async-start(bf16[32,2,8,2048]{3,2,1,0:T(8,128)(2,1)} %fold.1), calls=%async_computation | async-start | bytes 4194304 | tf_op jit(solution)/shard_map/all_to_all | solution.py:355
  19.6 2.5 %copy-start.2 = (s32[4]{0:T(128)}, s32[4]{0:T(128)S(1)}, u32[]{:S(2)}) copy-start(s32[4]{0:T(128)S(1)} %get-tuple-element.6.start_ref) | copy-start | bytes 52
  20.1 2.1 %copy-start.1 = (f32[6208]{0:T(1024)}, f32[6208]{0:T(1024)S(1)}, u32[]{:S(2)}) copy-start(f32[6208]{0:T(1024)S(1)} %sqrt.21.a_ref) | copy-start | bytes 74500
  47.9 1.3 %copy-start = (bf16[32,2,8,2048]{3,2,1,0:T(8,128)(2,1)}, bf16[32,2,8,2048]{3,2,1,0:T(8,128)(2,1)S(1)}, u32[]{:S(2)}) copy-start(bf16[32,2,8,2048]{3,2,1,0:T(8,128)(2,1)S(1)} %all-to-all-done) | copy-start | bytes 6291460
  59.1 53.9 %all-to-all-start.1 = ((bf16[256,24,128]{2,1,0:T(8,128)(2,1)}), bf16[256,24,128]{2,1,0:T(8,128)(2,1)S(1)}, u32[]{:S(2)}, u32[]{:S(2)}) async-start(bf16[256,24,128]{2,1,0:T(8,128)(2,1)} %bitcast.11), calls=%async_computation.1 | async-start | bytes 3145728 | tf_op jit(solution)/shard_map/all_to_all | solution.py:382
  72.2 5.3 %collective-permute-start = (bf16[6,512,256]{2,1,0:T(8,128)(2,1)S(1)}, bf16[6,512,256]{2,1,0:T(8,128)(2,1)S(1)}, u32[]{:S(2)}, u32[]{:S(2)}) collective-permute-start(bf16[6,512,256]{2,1,0:T(8,128)(2,1)S(1)} %dynamic-slice_bitcast_fusion), channel_id=1, source_target_pairs={{0,128},{128,0},{1,129},{129,1},{2,130},{130,2},{3,131},{131,3},{4... | collective-permute-start | bytes 4718600 | tf_op jit(solution)/shard_map/ppermute | solution.py:351

commit v3 on v2

--- a/solution.py
+++ b/solution.py
@@ -81,8 +81,8 @@
             pl.BlockSpec((1, 256, 2 * HALF), lambda s: (s, 0, 0)),
         ],
         out_specs=pl.BlockSpec((32, 1, 8, 2 * HALF), lambda s: (0, s, 0, 0)),
-        out_shape=jax.ShapeDtypeStruct((32, 2, 8, 2 * HALF), jnp.bfloat16),
-        compiler_params=pltpu.CompilerParams(vmem_limit_bytes=58 * 2**20),
+        out_shape=pltpu.HBM((32, 2, 8, 2 * HALF), jnp.bfloat16),
+        compiler_params=pltpu.CompilerParams(vmem_limit_bytes=16 * 2**20),
         name="fold",
     )(slots_pair, coeffs)
 
@@ -161,7 +161,7 @@
         out_specs=vmem,
         out_shape=jax.ShapeDtypeStruct((8, TABLE_ROWS, 128), jnp.bfloat16),
         scratch_shapes=[pltpu.VMEM((8 * TABLE_ROWS, 128), jnp.float32)],
-        compiler_params=pltpu.CompilerParams(vmem_limit_bytes=56 * 2**20),
+        compiler_params=pltpu.CompilerParams(vmem_limit_bytes=28 * 2**20),
         name="legendre",
     )(start, a_tab, ab_tab, cosine, weight, seed, level)
 
@@ -222,7 +222,7 @@
         transform_kernel,
         in_specs=[pl.BlockSpec(memory_space=pl.ANY), vmem],
         out_specs=pl.BlockSpec(memory_space=pltpu.HBM),
-        out_shape=jax.ShapeDtypeStruct((rows, 128), jnp.bfloat16),
+        out_shape=pltpu.HBM((rows, 128), jnp.bfloat16),
         scratch_shapes=[
             pltpu.VMEM((8, TABLE_ROWS, 128), jnp.bfloat16),
             pltpu.VMEM((CHAINS, 256, HALF), jnp.bfloat16),
@@ -230,9 +230,9 @@
             pltpu.VMEM((rows, 128), jnp.bfloat16),
             pltpu.SemaphoreType.DMA((2 * CHAINS + 2,)),
         ],
-        compiler_params=pltpu.CompilerParams(vmem_limit_bytes=54 * 2**20),
+        compiler_params=pltpu.CompilerParams(vmem_limit_bytes=24 * 2**20),
         name="transform",
-    )(table, x)
+    )(pltpu.with_memory_space_constraint(table, pltpu.HBM), x)
 
 
 def cross_kernel(who_ref, harm_ref, own_ref, other_ref, out_ref, wide):
@@ -295,9 +295,9 @@
             scratch_shapes=[pltpu.VMEM((256 * 24, 128), jnp.float32)],
         ),
         out_shape=jax.ShapeDtypeStruct((1, 6, 512, 512), jnp.float32),
-        compiler_params=pltpu.CompilerParams(vmem_limit_bytes=50 * 2**20),
+        compiler_params=pltpu.CompilerParams(vmem_limit_bytes=20 * 2**20),
         name="cross",
-    )(who, harmonic, bessel, partner)
+    )(who, harmonic, bessel, pltpu.with_memory_space_constraint(partner, pltpu.HBM))
 
 
 def cycle_geometry():

time: 122 us -> 116 us (0.951)
  Pallas kernels: 37.4 us -> 32.2 us
  waiting for transfers between devices: 48.8 us -> 51.4 us
  other arithmetic: 2.39 us -> 0.58 us
  local copies, waits for them, and re-layouts: 9.94 us -> 8.31 us
    pallas_call x1, Pallas kernels: 15.5 us -> 12.2 us  [legendre_tables(): pl.pallas_call(legendre_kernel, in_specs=[smem, smem, smem, vmem, vmem, v...]
    all_to_all x1, waiting for transfers between devices: 10.3 us -> 12.3 us  [per_device(): lax.all_to_all(folded, ('tracer', 'dev'), split_axis=0, concat_axis=0, ti...]
    dynamic_slice x1, local copies, waits for them, and re-layouts: 1.51 us -> 0.11 us  [per_device(): away = lax.dynamic_slice_in_dim(bessel[0], (1 - tracer) * 6, 6, 0)]
    pallas_call x1, Pallas kernels: 4.09 us -> 2.75 us  [fold_coefficients(): pl.pallas_call(fold_kernel, grid=(2,), in_specs=[pl.BlockSpec((1, 256), l...]
    unnamed x9 -> x7, local copies, waits for them, and re-layouts: 7.48 us -> 7.81 us
  transfers between devices with their start and end apart: 3 -> 3, of which waited for: 3 -> 3; matrix products, arithmetic and copies ran while one was open for 3% -> 1% of each run, Pallas kernels for 13% -> 11%
where the time goes in v3:
time: 116 us
  waiting for transfers between devices  51.4 us (44%)
  Pallas kernels  32.2 us (28%)
  starting transfers between devices  23.3 us (20%)
  local copies, waits for them, and re-layouts  8.31 us (7%)
    all_to_all x1, waiting for transfers between devices, per_device(): lax.all_to_all(harmonic.reshape(256, 24, 128), ('tracer', 'dev'), split_a...  36 us
    all_to_all x1, starting transfers between devices, per_device(): lax.all_to_all(harmonic.reshape(256, 24, 128), ('tracer', 'dev'), split_a...  12.4 us
    all_to_all x1, waiting for transfers between devices, per_device(): lax.all_to_all(folded, ('tracer', 'dev'), split_axis=0, concat_axis=0, ti...  12.3 us
    pallas_call x1, Pallas kernels, legendre_tables(): pl.pallas_call(legendre_kernel, in_specs=[smem, smem, smem, vmem, vmem, v...  12.2 us
    pallas_call x1, Pallas kernels, transform(): pl.pallas_call(transform_kernel, in_specs=[pl.BlockSpec(memory_space=pl.A...  8.64 us
    all_to_all x1, starting transfers between devices, per_device(): lax.all_to_all(folded, ('tracer', 'dev'), split_axis=0, concat_axis=0, ti...  8.58 us
    pallas_call x1, Pallas kernels, cross_spectrum(): pl.pallas_call(cross_kernel, grid_spec=pltpu.PrefetchScalarGridSpec(num_s...  8.56 us
    unnamed x7, local copies, waits for them, and re-layouts  7.81 us
  transfers between devices with their start and end apart: 3, of which 3 were waited for; matrix products, arithmetic and copies ran while one was open for 1% of the time, Pallas kernels for 11%

profile of v3, /device:TPU:1, one launch (start us, length us, event | category | flops | bytes accessed | tf_op | source)
XLA Modules:
  0.0 115.9 jit_solution(5273491115184733258)
XLA Ops:
  0.0 0.0 copy-start.2
  0.0 4.8 %copy.6 = bf16[1,2,256,2047]{3,2,1,0:T(8,128)(2,1)S(1)} copy(bf16[1,2,256,2047]{2,1,3,0:T(2,128)(2,1)} %param.3) | data formatting | bytes 4192256 | tf_op args[0]
  4.8 0.0 copy-done.2
  4.8 0.1 broadcast_in_dim.40
  4.8 0.1 broadcast_in_dim_reshape.3.slots_ref
  5.0 2.8 %fold.1 = bf16[32,2,8,2048]{3,2,1,0:T(8,128)(2,1)} custom-call(s32[1,256]{1,0:T(1,128)S(1)} %broadcast_in_dim_reshape.3.slots_ref, bf16[2,256,2047]{2,1,0:T(8,128)(2,1)S(1)} %bitcast.8), custom_call_target="tpu_custom_call" | custom-call | tf_op jit(solution)/shard_map/fold/pallas_call | solution.py:76
  7.8 8.6 %all-to-all-start = ((bf16[32,2,8,2048]{3,2,1,0:T(8,128)(2,1)}), bf16[32,2,8,2048]{3,2,1,0:T(8,128)(2,1)S(1)}, u32[]{:S(2)}, u32[]{:S(2)}) async-start(bf16[32,2,8,2048]{3,2,1,0:T(8,128)(2,1)} %fold.1), calls=%async_computation | async-start | bytes 4194304 | tf_op jit(solution)/shard_map/all_to_all | solution.py:355
  16.4 0.2 select_reduce_fusion
  16.6 0.1 divide_sqrt_fusion
  16.8 0.1 sqrt.21.a_ref
  16.8 0.1 sqrt.23
  17.0 0.1 floor_minimum_fusion
  17.1 12.2 %legendre.1.table_hbm = bf16[8,3840,128]{2,1,0:T(8,128)(2,1)S(1)} custom-call(s32[4]{0:T(128)S(1)} %get-tuple-element.6.start_ref, f32[6208]{0:T(1024)S(1)} %sqrt.21.a_ref, f32[6208]{0:T(1024)S(1)} %mul.174.ab_ref, f32[8,128]{1,0:T(8,128)S(1)} %get-tuple-element.20.cos_ref, f32[8,128]{1,0:T(8,128)S(1)} %get-tuple-element.19.weight_ref, ...), custom_call_target="tpu_custom_call" | custom-call | tf_op jit(solution)/shard_map/legendre/pallas_call | solution.py:158
  29.3 0.0 copy-start
  29.3 3.0 %copy-done = bf16[8,3840,128]{2,1,0:T(8,128)(2,1)} copy-done((bf16[8,3840,128]{2,1,0:T(8,128)(2,1)}, bf16[8,3840,128]{2,1,0:T(8,128)(2,1)S(1)}, u32[]{:S(2)}) %copy-start) | copy-done | bytes 7864344
  32.3 12.3 %all-to-all-done = bf16[32,2,8,2048]{3,2,1,0:T(8,128)(2,1)S(1)} async-done(((bf16[32,2,8,2048]{3,2,1,0:T(8,128)(2,1)}), bf16[32,2,8,2048]{3,2,1,0:T(8,128)(2,1)S(1)}, u32[]{:S(2)}, u32[]{:S(2)}) %all-to-all-start) | async-done | bytes 2097184 | tf_op jit(solution)/shard_map/all_to_all | solution.py:355
  44.7 8.6 %transform.1 = bf16[6144,128]{1,0:T(8,128)(2,1)} custom-call(bf16[8,3840,128]{2,1,0:T(8,128)(2,1)} %copy-done, bf16[512,2048]{1,0:T(8,128)(2,1)S(1)} %bitcast.9), custom_call_target="tpu_custom_call" | custom-call | tf_op jit(solution)/shard_map/transform/pallas_call | solution.py:221
  53.3 0.0 copy-start.1
  53.3 12.4 %all-to-all-start.1 = ((bf16[256,24,128]{2,1,0:T(8,128)(2,1)}), bf16[256,24,128]{2,1,0:T(8,128)(2,1)}, u32[]{:S(2)}, u32[]{:S(2)}) async-start(bf16[256,24,128]{2,1,0:T(8,128)(2,1)} %bitcast.10), calls=%async_computation.1 | async-start | bytes 3145728 | tf_op jit(solution)/shard_map/all_to_all | solution.py:382
  65.8 0.0 copy-done.1
  65.8 0.1 dynamic-slice_bitcast_fusion
  65.9 2.3 %collective-permute-start = (bf16[6,512,256]{2,1,0:T(8,128)(2,1)S(1)}, bf16[6,512,256]{2,1,0:T(8,128)(2,1)}, u32[]{:S(2)}, u32[]{:S(2)}) collective-permute-start(bf16[6,512,256]{2,1,0:T(8,128)(2,1)S(1)} %dynamic-slice_bitcast_fusion), channel_id=1, source_target_pairs={{0,128},{128,0},{1,129},{129,1},{2,130},{130,2},{3,131},{131,3},{4... | collective-permute-start | bytes 4718600 | tf_op jit(solution)/shard_map/ppermute | solution.py:351
  68.2 0.1 pad_add_fusion.who_ref
  68.3 3.1 %collective-permute-done.other_ref = bf16[6,512,256]{2,1,0:T(8,128)(2,1)} collective-permute-done((bf16[6,512,256]{2,1,0:T(8,128)(2,1)S(1)}, bf16[6,512,256]{2,1,0:T(8,128)(2,1)}, u32[]{:S(2)}, u32[]{:S(2)}) %collective-permute-start) | collective-permute-done | bytes 1572896 | tf_op jit(solution)/shard_map/ppermute | solution.py:351
  71.4 36.0 %all-to-all-done.1 = bf16[256,24,128]{2,1,0:T(8,128)(2,1)} async-done(((bf16[256,24,128]{2,1,0:T(8,128)(2,1)}), bf16[256,24,128]{2,1,0:T(8,128)(2,1)}, u32[]{:S(2)}, u32[]{:S(2)}) %all-to-all-start.1) | async-done | bytes 1572896 | tf_op jit(solution)/shard_map/all_to_all | solution.py:382
  107.3 8.6 %cross.1 = f32[1,6,512,512]{3,2,1,0:T(8,128)} custom-call(s32[2]{0:T(128)S(1)} %pad_add_fusion.who_ref, bf16[6144,128]{1,0:T(8,128)(2,1)} %bitcast.5.harm_ref, bf16[1,12,512,256]{3,2,1,0:T(8,128)(2,1)S(1)} %copy-done.1, bf16[6,512,256]{2,1,0:T(8,128)(2,1)} %collective-permute-done.other_ref), custom_call_target="tpu_custom_call" | custom-call | tf_op jit(solution)/shard_map/cross/pallas_call | solution.py:284
  (8 shorter events, 0.1 us)
Async XLA Ops:
  0.0 4.8 %copy-start.2 = (s32[128]{0:T(128)S(1)}, s32[128]{0:T(128)}, u32[]{:S(2)}) copy-start(s32[128]{0:T(128)} %param.5) | copy-start | bytes 1540
  7.8 36.9 %all-to-all-start = ((bf16[32,2,8,2048]{3,2,1,0:T(8,128)(2,1)}), bf16[32,2,8,2048]{3,2,1,0:T(8,128)(2,1)S(1)}, u32[]{:S(2)}, u32[]{:S(2)}) async-start(bf16[32,2,8,2048]{3,2,1,0:T(8,128)(2,1)} %fold.1), calls=%async_computation | async-start | bytes 4194304 | tf_op jit(solution)/shard_map/all_to_all | solution.py:355
  29.3 3.0 %copy-start = (bf16[8,3840,128]{2,1,0:T(8,128)(2,1)}, bf16[8,3840,128]{2,1,0:T(8,128)(2,1)S(1)}, u32[]{:S(2)}) copy-start(bf16[8,3840,128]{2,1,0:T(8,128)(2,1)S(1)} %legendre.1.table_hbm) | copy-start | bytes 23592964
  53.3 12.5 %copy-start.1 = (bf16[1,12,512,256]{3,2,1,0:T(8,128)(2,1)S(1)}, bf16[1,12,512,256]{3,2,1,0:T(8,128)(2,1)}, u32[]{:S(2)}) copy-start(bf16[1,12,512,256]{3,2,1,0:T(8,128)(2,1)} %own_ref.1) | copy-start | bytes 9437188
  53.3 54.0 %all-to-all-start.1 = ((bf16[256,24,128]{2,1,0:T(8,128)(2,1)}), bf16[256,24,128]{2,1,0:T(8,128)(2,1)}, u32[]{:S(2)}, u32[]{:S(2)}) async-start(bf16[256,24,128]{2,1,0:T(8,128)(2,1)} %bitcast.10), calls=%async_computation.1 | async-start | bytes 3145728 | tf_op jit(solution)/shard_map/all_to_all | solution.py:382
  65.9 5.5 %collective-permute-start = (bf16[6,512,256]{2,1,0:T(8,128)(2,1)S(1)}, bf16[6,512,256]{2,1,0:T(8,128)(2,1)}, u32[]{:S(2)}, u32[]{:S(2)}) collective-permute-start(bf16[6,512,256]{2,1,0:T(8,128)(2,1)S(1)} %dynamic-slice_bitcast_fusion), channel_id=1, source_target_pairs={{0,128},{128,0},{1,129},{129,1},{2,130},{130,2},{3,131},{131,3},{4... | collective-permute-start | bytes 4718600 | tf_op jit(solution)/shard_map/ppermute | solution.py:351

commit v4 on v3

--- a/solution.py
+++ b/solution.py
@@ -15,6 +15,8 @@
 OWNERS = 128
 TABLE = LMAX + 16
 CHAINS = 4
+DEGREES_STEP = 2
+CHUNK = 384
 SPREAD = OWNERS // CHAINS
 BLOCK_ROWS = 6 * SPREAD
 STEP_LOG2 = 64.0
@@ -40,21 +42,14 @@
     return SPREAD * j + jnp.where(flip == 0, place, SPREAD - 1 - place)
 
 
-def fold_kernel(slots_ref, coef_ref, out_ref):
+def fold_kernel(coef_ref, out_ref):
     x = coef_ref[0]
-    row = lax.broadcasted_iota(jnp.int32, (256, 256), 0)
-    col = lax.broadcasted_iota(jnp.int32, (256, 256), 1)
-    member = row // 8
-    j = (row % 8) // 2
-    place = jnp.where(j % 2 == 0, member, SPREAD - 1 - member)
-    wanted = STRIDE * (SPREAD * j + place)
-    hit = jnp.logical_and(slots_ref[...] == wanted, row % 2 == col % 2)
-    pick = jnp.where(hit, 1.0, 0.0).astype(jnp.bfloat16)
-    south = x[:, HALF:].astype(jnp.float32)
-    lane = lax.broadcasted_iota(jnp.int32, south.shape, 1)
-    south = jnp.where(lane < HALF - 1, south, 0.0).astype(jnp.bfloat16)
-    north = jnp.dot(pick, x[:, :HALF], preferred_element_type=jnp.float32)
-    south = jnp.dot(pick, south, preferred_element_type=jnp.float32).astype(jnp.bfloat16)
+    north = x[:, :HALF].astype(jnp.float32)
+    south = x[:, HALF:]
+    edge = south[:, HALF - 128 :].astype(jnp.float32)
+    lane = lax.broadcasted_iota(jnp.int32, edge.shape, 1)
+    edge = jnp.where(lane < 127, edge, 0.0).astype(jnp.bfloat16)
+    south = jnp.concatenate([south[:, : HALF - 128], edge], axis=1)
     back_row = lax.broadcasted_iota(jnp.int32, (256, 128), 0)
     back_col = lax.broadcasted_iota(jnp.int32, (256, 128), 1)
     back = jnp.where(back_row + back_col == 254, 1.0, 0.0).astype(jnp.bfloat16)
@@ -72,19 +67,26 @@
         out_ref[:, 0, :, HALF + 128 * b : HALF + 128 * (b + 1)] = odd.reshape(32, 8, 128)
 
 
-def fold_coefficients(slots_pair, coeffs):
+def fold_coefficients(slots, coeffs):
+    row = jnp.arange(256, dtype=jnp.int32)
+    j = (row % 8) // 2
+    place = jnp.where(j % 2 == 0, row // 8, SPREAD - 1 - row // 8)
+    wanted = STRIDE * (SPREAD * j + place)
+    hit = jnp.logical_and(
+        jnp.repeat(slots, 2)[None, :] == wanted[:, None], row[None, :] % 2 == row[:, None] % 2
+    )
+    picked = jnp.einsum(
+        "pr,src->spc", hit.astype(jnp.bfloat16), coeffs, preferred_element_type=jnp.float32
+    ).astype(jnp.bfloat16)
     return pl.pallas_call(
         fold_kernel,
         grid=(2,),
-        in_specs=[
-            pl.BlockSpec((1, 256), lambda s: (0, 0)),
-            pl.BlockSpec((1, 256, 2 * HALF), lambda s: (s, 0, 0)),
-        ],
+        in_specs=[pl.BlockSpec((1, 256, 2 * HALF), lambda s: (s, 0, 0))],
         out_specs=pl.BlockSpec((32, 1, 8, 2 * HALF), lambda s: (0, s, 0, 0)),
         out_shape=pltpu.HBM((32, 2, 8, 2 * HALF), jnp.bfloat16),
         compiler_params=pltpu.CompilerParams(vmem_limit_bytes=16 * 2**20),
         name="fold",
-    )(slots_pair, coeffs)
+    )(picked)
 
 
 def legendre_kernel(
@@ -192,20 +194,22 @@
     contract = (((1,), (1,)), ((), ()))
     for h in range(2):
         for j in range(CHAINS):
-            both = picked[j]
             copies[CHAINS * h + j].wait()
-            first = table_base(j) + h * half_rows(j)
-            last = first + half_rows(j)
-            rows = jnp.concatenate([table[s, first:last, :] for s in range(8)], axis=1)
-            got = lax.dot_general(rows, both, contract, preferred_element_type=jnp.float32)
-            parity = lax.broadcasted_iota(jnp.int32, (half_rows(j), 128), 0) % 2
+            gap = BLOCK_ROWS * j
             base = h * 4 * half_rows(0) + j
-            gap = BLOCK_ROWS * j
             if gap:
                 wide[pl.ds(base, gap, stride=4), :] = jnp.zeros((gap, 128), jnp.float32)
-            wide[pl.ds(base + 4 * gap, half_rows(j), stride=4), :] = jnp.where(
-                parity == 0, got[:, :128], got[:, 128:]
-            )
+            for done in range(0, half_rows(j), CHUNK):
+                size = min(CHUNK, half_rows(j) - done)
+                first = table_base(j) + h * half_rows(j) + done
+                rows = jnp.concatenate(
+                    [table[s, first : first + size, :] for s in range(8)], axis=1
+                )
+                got = lax.dot_general(rows, picked[j], contract, preferred_element_type=jnp.float32)
+                parity = lax.broadcasted_iota(jnp.int32, (size, 128), 0) % 2
+                wide[pl.ds(base + 4 * (gap + done), size, stride=4), :] = jnp.where(
+                    parity == 0, got[:, :128], got[:, 128:]
+                )
         half = pl.ds(h * 4 * half_rows(0), 4 * half_rows(0))
         packed[half, :] = wide[half, :].astype(jnp.bfloat16)
         copy = pltpu.make_async_copy(packed.at[half], out_hbm.at[half], sems.at[2 * CHAINS + h])
@@ -235,15 +239,8 @@
     )(pltpu.with_memory_space_constraint(table, pltpu.HBM), x)
 
 
-def cross_kernel(who_ref, harm_ref, own_ref, other_ref, out_ref, wide):
-    i = pl.program_id(0)
-
-    @pl.when(i == 0)
-    def _():
-        wide[...] = harm_ref[...].astype(jnp.float32)
-
-    tracer, owner = who_ref[0], who_ref[1]
-    lane = lax.broadcasted_iota(jnp.int32, (16, 128), 1) // 32
+def degree_fields(wide, i):
+    lane = lax.broadcasted_iota(jnp.int32, (PLANE, 128), 1) // 32
     blocks = [[], []]
     for core in range(2):
         for j in range(CHAINS):
@@ -265,39 +262,64 @@
                 blocks[part // 2].append(
                     jnp.concatenate(tiles[part], axis=1).astype(jnp.bfloat16)
                 )
-    fields = [jnp.concatenate(rows, axis=0) for rows in blocks]
-    own, other = own_ref[0, 0], other_ref[0]
+    return [jnp.concatenate(rows, axis=0) for rows in blocks]
+
+
+def cross_kernel(who_ref, harm_ref, own_ref, other_ref, out_ref, wide):
+    step = pl.program_id(0)
+
+    @pl.when(step == 0)
+    def _():
+        wide[...] = harm_ref[...].astype(jnp.float32)
+
+    tracer, owner = who_ref[0], who_ref[1]
     first = tracer == 0
-    basis_lead = jnp.where(first, own, other)
-    basis_trail = jnp.where(first, other, own)
+    tally = jnp.full((1, 512), owner + 1, jnp.int32).astype(jnp.float32)
+    factor = 1.0 / jnp.sqrt(2.0 * tally)
     contract = (((1,), (1,)), ((), ()))
-    lead = lax.dot_general(basis_lead, fields[0], contract, preferred_element_type=jnp.float32)
-    trail = lax.dot_general(fields[1], basis_trail, contract, preferred_element_type=jnp.float32)
-    total = jnp.dot(
-        lead.astype(jnp.bfloat16), trail.astype(jnp.bfloat16), preferred_element_type=jnp.float32
-    )
-    tally = jnp.full((1, 512), owner + 1, jnp.int32).astype(jnp.float32)
-    out_ref[0, 0] = total * (1.0 / jnp.sqrt(2.0 * tally))
+    for e in range(DEGREES_STEP):
+        fields = degree_fields(wide, DEGREES_STEP * step + e)
+        own, other = own_ref[0, e], other_ref[e]
+        basis_lead = jnp.where(first, own, other)
+        basis_trail = jnp.where(first, other, own)
+        lead = lax.dot_general(basis_lead, fields[0], contract, preferred_element_type=jnp.float32)
+        trail = lax.dot_general(
+            fields[1], basis_trail, contract, preferred_element_type=jnp.float32
+        )
+        total = jnp.dot(
+            lead.astype(jnp.bfloat16),
+            trail.astype(jnp.bfloat16),
+            preferred_element_type=jnp.float32,
+        )
+        out_ref[0, e] = total * factor
 
 
 def cross_spectrum(who, harmonic, bessel, partner):
+    steps = 6 // DEGREES_STEP
     return pl.pallas_call(
         cross_kernel,
         grid_spec=pltpu.PrefetchScalarGridSpec(
             num_scalar_prefetch=1,
-            grid=(6,),
+            grid=(steps,),
             in_specs=[
                 pl.BlockSpec((256 * 24, 128), lambda i, who: (0, 0)),
-                pl.BlockSpec((1, 1, 512, 256), lambda i, who: (0, 6 * who[0] + i, 0, 0)),
-                pl.BlockSpec((1, 512, 256), lambda i, who: (i, 0, 0)),
+                pl.BlockSpec(
+                    (1, DEGREES_STEP, 512, 256), lambda i, who: (0, steps * who[0] + i, 0, 0)
+                ),
+                pl.BlockSpec((DEGREES_STEP, 512, 256), lambda i, who: (i, 0, 0)),
             ],
-            out_specs=pl.BlockSpec((1, 1, 512, 512), lambda i, who: (0, i, 0, 0)),
+            out_specs=pl.BlockSpec((1, DEGREES_STEP, 512, 512), lambda i, who: (0, i, 0, 0)),
             scratch_shapes=[pltpu.VMEM((256 * 24, 128), jnp.float32)],
         ),
         out_shape=jax.ShapeDtypeStruct((1, 6, 512, 512), jnp.float32),
-        compiler_params=pltpu.CompilerParams(vmem_limit_bytes=20 * 2**20),
+        compiler_params=pltpu.CompilerParams(vmem_limit_bytes=24 * 2**20),
         name="cross",
-    )(who, harmonic, bessel, pltpu.with_memory_space_constraint(partner, pltpu.HBM))
+    )(
+        who,
+        harmonic,
+        pltpu.with_memory_space_constraint(bessel, pltpu.HBM),
+        pltpu.with_memory_space_constraint(partner, pltpu.HBM),
+    )
 
 
 def cycle_geometry():
@@ -350,8 +372,7 @@
     away = lax.dynamic_slice_in_dim(bessel[0], (1 - tracer) * 6, 6, 0)
     partner = lax.ppermute(away, "tracer", [(0, 1), (1, 0)])
 
-    slots_pair = jnp.repeat(azimuthal_order_slots, 2)[None, :]
-    folded = fold_coefficients(slots_pair, coeffs[0])
+    folded = fold_coefficients(azimuthal_order_slots, coeffs[0])
     regrouped = lax.all_to_all(
         folded,
         ("tracer", "dev"),

time: 116 us -> 112 us (0.966)
  local copies, waits for them, and re-layouts: 8.31 us -> 6.32 us
  Pallas kernels: 32.2 us -> 30.6 us
  waiting for transfers between devices: 51.4 us -> 50 us
    unnamed x7 -> x4, local copies, waits for them, and re-layouts: 7.81 us -> 3.61 us
    dynamic_slice x1, local copies, waits for them, and re-layouts: 0.11 us -> 1.51 us  [per_device(): away = lax.dynamic_slice_in_dim(bessel[0], (1 - tracer) * 6, 6, 0)]
    all_to_all x1, waiting for transfers between devices: 36 us -> 34.6 us  [per_device(): lax.all_to_all(harmonic.reshape(256, 24, 128), ('tracer', 'dev'), split_a...]
  transfers between devices with their start and end apart: 3 -> 3, of which waited for: 3 -> 3; matrix products, arithmetic and copies ran while one was open for 1% -> 2% of each run, Pallas kernels for 11% -> 11%
where the time goes in v4:
time: 112 us
  waiting for transfers between devices  50 us (45%)
  Pallas kernels  30.6 us (27%)
  starting transfers between devices  23.4 us (21%)
  local copies, waits for them, and re-layouts  6.32 us (6%)
    all_to_all x1, waiting for transfers between devices, per_device(): lax.all_to_all(harmonic.reshape(256, 24, 128), ('tracer', 'dev'), split_a...  34.6 us
    all_to_all x1, starting transfers between devices, per_device(): lax.all_to_all(harmonic.reshape(256, 24, 128), ('tracer', 'dev'), split_a...  12.4 us
    all_to_all x1, waiting for transfers between devices, per_device(): lax.all_to_all(folded, ('tracer', 'dev'), split_axis=0, concat_axis=0, ti...  12.4 us
    pallas_call x1, Pallas kernels, legendre_tables(): pl.pallas_call(legendre_kernel, in_specs=[smem, smem, smem, vmem, vmem, v...  12.2 us
    all_to_all x1, starting transfers between devices, per_device(): lax.all_to_all(folded, ('tracer', 'dev'), split_axis=0, concat_axis=0, ti...  8.64 us
    pallas_call x1, Pallas kernels, transform(): pl.pallas_call(transform_kernel, in_specs=[pl.BlockSpec(memory_space=pl.A...  8.59 us
    pallas_call x1, Pallas kernels, cross_spectrum(): pl.pallas_call(cross_kernel, grid_spec=pltpu.PrefetchScalarGridSpec(num_s...  7.99 us
    unnamed x4, local copies, waits for them, and re-layouts  3.61 us
  transfers between devices with their start and end apart: 3, of which 3 were waited for; matrix products, arithmetic and copies ran while one was open for 2% of the time, Pallas kernels for 11%

profile of v4, /device:TPU:1, one launch (start us, length us, event | category | flops | bytes accessed | tf_op | source)
XLA Modules:
  0.0 111.8 jit_solution(9884062091102814152)
XLA Ops:
  0.0 0.0 copy-start
  0.0 0.9 broadcast_in_dim.43
  0.9 0.1 eq.57
  1.0 0.6 copy-done
  1.6 0.8 fusion.coef_ref
  2.4 1.9 %fold.1 = bf16[32,2,8,2048]{3,2,1,0:T(8,128)(2,1)} custom-call(bf16[2,256,2047]{2,1,0:T(8,128)(2,1)S(1)} %fusion.coef_ref), custom_call_target="tpu_custom_call" | custom-call | tf_op jit(solution)/shard_map/fold/pallas_call | solution.py:81
  4.2 8.6 %all-to-all-start = ((bf16[32,2,8,2048]{3,2,1,0:T(8,128)(2,1)}), bf16[32,2,8,2048]{3,2,1,0:T(8,128)(2,1)}, u32[]{:S(2)}, u32[]{:S(2)}) async-start(bf16[32,2,8,2048]{3,2,1,0:T(8,128)(2,1)} %fold.1), calls=%async_computation | async-start | bytes 4194304 | tf_op jit(solution)/shard_map/all_to_all | solution.py:376
  13.0 0.2 select_reduce_fusion
  13.2 0.1 divide_sqrt_fusion
  13.3 0.1 sqrt.21.a_ref
  13.4 0.1 sqrt.23
  13.5 0.1 floor_minimum_fusion
  13.6 12.2 %legendre.1.table_hbm = bf16[8,3840,128]{2,1,0:T(8,128)(2,1)S(1)} custom-call(s32[4]{0:T(128)S(1)} %get-tuple-element.6.start_ref, f32[6208]{0:T(1024)S(1)} %sqrt.21.a_ref, f32[6208]{0:T(1024)S(1)} %mul.194.ab_ref, f32[8,128]{1,0:T(8,128)S(1)} %get-tuple-element.20.cos_ref, f32[8,128]{1,0:T(8,128)S(1)} %get-tuple-element.19.weight_ref, ...), custom_call_target="tpu_custom_call" | custom-call | tf_op jit(solution)/shard_map/legendre/pallas_call | solution.py:160
  25.8 0.0 copy-start.1
  25.8 3.0 %copy-done.1 = bf16[8,3840,128]{2,1,0:T(8,128)(2,1)} copy-done((bf16[8,3840,128]{2,1,0:T(8,128)(2,1)}, bf16[8,3840,128]{2,1,0:T(8,128)(2,1)S(1)}, u32[]{:S(2)}) %copy-start.1) | copy-done | bytes 7864344
  28.9 12.4 %all-to-all-done = bf16[32,2,8,2048]{3,2,1,0:T(8,128)(2,1)} async-done(((bf16[32,2,8,2048]{3,2,1,0:T(8,128)(2,1)}), bf16[32,2,8,2048]{3,2,1,0:T(8,128)(2,1)}, u32[]{:S(2)}, u32[]{:S(2)}) %all-to-all-start) | async-done | bytes 2097184 | tf_op jit(solution)/shard_map/all_to_all | solution.py:376
  41.2 8.6 %transform.1 = bf16[6144,128]{1,0:T(8,128)(2,1)} custom-call(bf16[8,3840,128]{2,1,0:T(8,128)(2,1)} %copy-done.1, bf16[512,2048]{1,0:T(8,128)(2,1)} %bitcast.5.x_ref), custom_call_target="tpu_custom_call" | custom-call | tf_op jit(solution)/shard_map/transform/pallas_call | solution.py:225
  49.8 12.4 %all-to-all-start.1 = ((bf16[256,24,128]{2,1,0:T(8,128)(2,1)}), bf16[256,24,128]{2,1,0:T(8,128)(2,1)}, u32[]{:S(2)}, u32[]{:S(2)}) async-start(bf16[256,24,128]{2,1,0:T(8,128)(2,1)} %bitcast.14), calls=%async_computation.1 | async-start | bytes 3145728 | tf_op jit(solution)/shard_map/all_to_all | solution.py:403
  62.3 1.5 %dynamic-slice_bitcast_fusion = bf16[6,512,256]{2,1,0:T(8,128)(2,1)S(1)} fusion(bf16[1,12,512,256]{3,2,1,0:T(8,128)(2,1)} %own_ref.1, s32[]{:T(128)S(6)} %select_n.118), kind=kLoop, calls=%fused_computation.3 | loop fusion | bytes 3145732 | tf_op jit(solution)/shard_map/dynamic_slice | solution.py:372
  63.8 2.3 %collective-permute-start = (bf16[6,512,256]{2,1,0:T(8,128)(2,1)S(1)}, bf16[6,512,256]{2,1,0:T(8,128)(2,1)}, u32[]{:S(2)}, u32[]{:S(2)}) collective-permute-start(bf16[6,512,256]{2,1,0:T(8,128)(2,1)S(1)} %dynamic-slice_bitcast_fusion), channel_id=1, source_target_pairs={{0,128},{128,0},{1,129},{129,1},{2,130},{130,2},{3,131},{131,3},{4... | collective-permute-start | bytes 4718600 | tf_op jit(solution)/shard_map/ppermute | solution.py:373
  66.1 0.1 pad_add_fusion.who_ref
  66.2 3.1 %collective-permute-done.other_ref = bf16[6,512,256]{2,1,0:T(8,128)(2,1)} collective-permute-done((bf16[6,512,256]{2,1,0:T(8,128)(2,1)S(1)}, bf16[6,512,256]{2,1,0:T(8,128)(2,1)}, u32[]{:S(2)}, u32[]{:S(2)}) %collective-permute-start) | collective-permute-done | bytes 1572896 | tf_op jit(solution)/shard_map/ppermute | solution.py:373
  69.3 34.6 %all-to-all-done.1 = bf16[256,24,128]{2,1,0:T(8,128)(2,1)} async-done(((bf16[256,24,128]{2,1,0:T(8,128)(2,1)}), bf16[256,24,128]{2,1,0:T(8,128)(2,1)}, u32[]{:S(2)}, u32[]{:S(2)}) %all-to-all-start.1) | async-done | bytes 1572896 | tf_op jit(solution)/shard_map/all_to_all | solution.py:403
  103.9 8.0 %cross.1 = f32[1,6,512,512]{3,2,1,0:T(8,128)} custom-call(s32[2]{0:T(128)S(1)} %pad_add_fusion.who_ref, bf16[6144,128]{1,0:T(8,128)(2,1)} %bitcast.7.harm_ref, bf16[1,12,512,256]{3,2,1,0:T(8,128)(2,1)} %own_ref.1, bf16[6,512,256]{2,1,0:T(8,128)(2,1)} %collective-permute-done.other_ref), custom_call_target="tpu_custom_call" | custom-call | tf_op jit(solution)/shard_map/cross/pallas_call | solution.py:299
  (9 shorter events, 0.1 us)
Async XLA Ops:
  0.0 1.6 %copy-start = (bf16[1,2,256,2047]{2,1,3,0:T(2,128)(2,1)S(1)}, bf16[1,2,256,2047]{2,1,3,0:T(2,128)(2,1)}, u32[]{:S(2)}) copy-start(bf16[1,2,256,2047]{2,1,3,0:T(2,128)(2,1)} %param.3) | copy-start | bytes 6288388
  4.2 37.0 %all-to-all-start = ((bf16[32,2,8,2048]{3,2,1,0:T(8,128)(2,1)}), bf16[32,2,8,2048]{3,2,1,0:T(8,128)(2,1)}, u32[]{:S(2)}, u32[]{:S(2)}) async-start(bf16[32,2,8,2048]{3,2,1,0:T(8,128)(2,1)} %fold.1), calls=%async_computation | async-start | bytes 4194304 | tf_op jit(solution)/shard_map/all_to_all | solution.py:376
  25.8 3.0 %copy-start.1 = (bf16[8,3840,128]{2,1,0:T(8,128)(2,1)}, bf16[8,3840,128]{2,1,0:T(8,128)(2,1)S(1)}, u32[]{:S(2)}) copy-start(bf16[8,3840,128]{2,1,0:T(8,128)(2,1)S(1)} %legendre.1.table_hbm) | copy-start | bytes 23592964
  49.8 54.0 %all-to-all-start.1 = ((bf16[256,24,128]{2,1,0:T(8,128)(2,1)}), bf16[256,24,128]{2,1,0:T(8,128)(2,1)}, u32[]{:S(2)}, u32[]{:S(2)}) async-start(bf16[256,24,128]{2,1,0:T(8,128)(2,1)} %bitcast.14), calls=%async_computation.1 | async-start | bytes 3145728 | tf_op jit(solution)/shard_map/all_to_all | solution.py:403
  63.8 5.5 %collective-permute-start = (bf16[6,512,256]{2,1,0:T(8,128)(2,1)S(1)}, bf16[6,512,256]{2,1,0:T(8,128)(2,1)}, u32[]{:S(2)}, u32[]{:S(2)}) collective-permute-start(bf16[6,512,256]{2,1,0:T(8,128)(2,1)S(1)} %dynamic-slice_bitcast_fusion), channel_id=1, source_target_pairs={{0,128},{128,0},{1,129},{129,1},{2,130},{130,2},{3,131},{131,3},{4... | collective-permute-start | bytes 4718600 | tf_op jit(solution)/shard_map/ppermute | solution.py:373

commit v5 on v4

--- a/solution.py
+++ b/solution.py
@@ -15,7 +15,7 @@
 OWNERS = 128
 TABLE = LMAX + 16
 CHAINS = 4
-DEGREES_STEP = 2
+DEGREES = 6
 CHUNK = 384
 SPREAD = OWNERS // CHAINS
 BLOCK_ROWS = 6 * SPREAD
@@ -168,7 +168,15 @@
     )(start, a_tab, ab_tab, cosine, weight, seed, level)
 
 
-def transform_kernel(table_hbm, x_ref, out_hbm, table, picked, wide, packed, sems):
+def transform_kernel(table_hbm, x_hbm, out_hbm, table, x_ref, picked, wide, packed, sems):
+    loads = []
+    for t in range(2):
+        span = pl.ds(256 * t, 256)
+        copy = pltpu.make_async_copy(
+            x_hbm.at[span], x_ref.at[span], sems.at[2 * CHAINS + 2 + t]
+        )
+        copy.start()
+        loads.append(copy)
     copies = []
     for h in range(2):
         for j in range(CHAINS):
@@ -183,6 +191,8 @@
     shell = row % 32
     source = (shell // 2) * 16 + (shell % 2) * 8 + (row // 64) * 2 + (row % 64) // 32
     pick = jnp.where(source == col, 1.0, 0.0).astype(jnp.bfloat16)
+    for copy in loads:
+        copy.wait()
     for t in range(2):
         got = jnp.dot(
             pick, x_ref[256 * t : 256 * (t + 1), :], preferred_element_type=jnp.float32
@@ -195,6 +205,7 @@
     for h in range(2):
         for j in range(CHAINS):
             copies[CHAINS * h + j].wait()
+        for j in range(CHAINS):
             gap = BLOCK_ROWS * j
             base = h * 4 * half_rows(0) + j
             if gap:
@@ -221,22 +232,26 @@
 
 def transform(table, x):
     rows = 8 * half_rows(0)
-    vmem = pl.BlockSpec(memory_space=pltpu.VMEM)
+    hbm = pl.BlockSpec(memory_space=pl.ANY)
     return pl.pallas_call(
         transform_kernel,
-        in_specs=[pl.BlockSpec(memory_space=pl.ANY), vmem],
+        in_specs=[hbm, hbm],
         out_specs=pl.BlockSpec(memory_space=pltpu.HBM),
         out_shape=pltpu.HBM((rows, 128), jnp.bfloat16),
         scratch_shapes=[
             pltpu.VMEM((8, TABLE_ROWS, 128), jnp.bfloat16),
+            pltpu.VMEM((512, 2 * HALF), jnp.bfloat16),
             pltpu.VMEM((CHAINS, 256, HALF), jnp.bfloat16),
             pltpu.VMEM((rows, 128), jnp.float32),
             pltpu.VMEM((rows, 128), jnp.bfloat16),
-            pltpu.SemaphoreType.DMA((2 * CHAINS + 2,)),
+            pltpu.SemaphoreType.DMA((2 * CHAINS + 4,)),
         ],
         compiler_params=pltpu.CompilerParams(vmem_limit_bytes=24 * 2**20),
         name="transform",
-    )(pltpu.with_memory_space_constraint(table, pltpu.HBM), x)
+    )(
+        pltpu.with_memory_space_constraint(table, pltpu.HBM),
+        pltpu.with_memory_space_constraint(x, pltpu.HBM),
+    )
 
 
 def degree_fields(wide, i):
@@ -265,58 +280,86 @@
     return [jnp.concatenate(rows, axis=0) for rows in blocks]
 
 
-def cross_kernel(who_ref, harm_ref, own_ref, other_ref, out_ref, wide):
-    step = pl.program_id(0)
-
-    @pl.when(step == 0)
-    def _():
-        wide[...] = harm_ref[...].astype(jnp.float32)
-
+def cross_kernel(
+    who_ref, harm_hbm, own_hbm, other_hbm, out_hbm, harm, wide, own, other, out, sems
+):
     tracer, owner = who_ref[0], who_ref[1]
+    part = OWNERS * 24
+    arrivals = []
+    for core in range(2):
+        span = pl.ds(core * part, part)
+        arrivals.append(pltpu.make_async_copy(harm_hbm.at[span], harm.at[span], sems.at[core]))
+    for e in range(DEGREES):
+        arrivals.append(
+            pltpu.make_async_copy(own_hbm.at[0, DEGREES * tracer + e], own.at[e], sems.at[2 + e])
+        )
+        arrivals.append(
+            pltpu.make_async_copy(other_hbm.at[e], other.at[e], sems.at[2 + DEGREES + e])
+        )
+    for copy in arrivals:
+        copy.start()
+    for core in range(2):
+        arrivals[core].wait()
+        span = pl.ds(core * part, part)
+        wide[span, :] = harm[span, :].astype(jnp.float32)
     first = tracer == 0
     tally = jnp.full((1, 512), owner + 1, jnp.int32).astype(jnp.float32)
     factor = 1.0 / jnp.sqrt(2.0 * tally)
     contract = (((1,), (1,)), ((), ()))
-    for e in range(DEGREES_STEP):
-        fields = degree_fields(wide, DEGREES_STEP * step + e)
-        own, other = own_ref[0, e], other_ref[e]
-        basis_lead = jnp.where(first, own, other)
-        basis_trail = jnp.where(first, other, own)
-        lead = lax.dot_general(basis_lead, fields[0], contract, preferred_element_type=jnp.float32)
-        trail = lax.dot_general(
-            fields[1], basis_trail, contract, preferred_element_type=jnp.float32
-        )
-        total = jnp.dot(
-            lead.astype(jnp.bfloat16),
-            trail.astype(jnp.bfloat16),
-            preferred_element_type=jnp.float32,
-        )
-        out_ref[0, e] = total * factor
+    departures = []
+    for e0 in range(0, DEGREES, 3):
+        group = range(e0, e0 + 3)
+        for e in group:
+            arrivals[2 + 2 * e].wait()
+            arrivals[3 + 2 * e].wait()
+        for e in group:
+            fields = degree_fields(wide, e)
+            mine, theirs = own[e], other[e]
+            basis_lead = jnp.where(first, mine, theirs)
+            basis_trail = jnp.where(first, theirs, mine)
+            lead = lax.dot_general(
+                basis_lead, fields[0], contract, preferred_element_type=jnp.float32
+            )
+            trail = lax.dot_general(
+                fields[1], basis_trail, contract, preferred_element_type=jnp.float32
+            )
+            total = jnp.dot(
+                lead.astype(jnp.bfloat16),
+                trail.astype(jnp.bfloat16),
+                preferred_element_type=jnp.float32,
+            )
+            out[e] = total * factor
+        for e in group:
+            copy = pltpu.make_async_copy(
+                out.at[e], out_hbm.at[0, e], sems.at[2 + 2 * DEGREES + e]
+            )
+            copy.start()
+            departures.append(copy)
+    for copy in departures:
+        copy.wait()
 
 
 def cross_spectrum(who, harmonic, bessel, partner):
-    steps = 6 // DEGREES_STEP
+    hbm = pl.BlockSpec(memory_space=pl.ANY)
+    rows = 2 * OWNERS * 24
     return pl.pallas_call(
         cross_kernel,
-        grid_spec=pltpu.PrefetchScalarGridSpec(
-            num_scalar_prefetch=1,
-            grid=(steps,),
-            in_specs=[
-                pl.BlockSpec((256 * 24, 128), lambda i, who: (0, 0)),
-                pl.BlockSpec(
-                    (1, DEGREES_STEP, 512, 256), lambda i, who: (0, steps * who[0] + i, 0, 0)
-                ),
-                pl.BlockSpec((DEGREES_STEP, 512, 256), lambda i, who: (i, 0, 0)),
-            ],
-            out_specs=pl.BlockSpec((1, DEGREES_STEP, 512, 512), lambda i, who: (0, i, 0, 0)),
-            scratch_shapes=[pltpu.VMEM((256 * 24, 128), jnp.float32)],
-        ),
-        out_shape=jax.ShapeDtypeStruct((1, 6, 512, 512), jnp.float32),
-        compiler_params=pltpu.CompilerParams(vmem_limit_bytes=24 * 2**20),
+        in_specs=[pl.BlockSpec(memory_space=pltpu.SMEM), hbm, hbm, hbm],
+        out_specs=hbm,
+        out_shape=jax.ShapeDtypeStruct((1, DEGREES, 512, 512), jnp.float32),
+        scratch_shapes=[
+            pltpu.VMEM((rows, 128), jnp.bfloat16),
+            pltpu.VMEM((rows, 128), jnp.float32),
+            pltpu.VMEM((DEGREES, 512, 256), jnp.bfloat16),
+            pltpu.VMEM((DEGREES, 512, 256), jnp.bfloat16),
+            pltpu.VMEM((DEGREES, 512, 512), jnp.float32),
+            pltpu.SemaphoreType.DMA((2 + 3 * DEGREES,)),
+        ],
+        compiler_params=pltpu.CompilerParams(vmem_limit_bytes=32 * 2**20),
         name="cross",
     )(
         who,
-        harmonic,
+        pltpu.with_memory_space_constraint(harmonic, pltpu.HBM),
         pltpu.with_memory_space_constraint(bessel, pltpu.HBM),
         pltpu.with_memory_space_constraint(partner, pltpu.HBM),
     )

time: 112 us -> 109 us (0.973)
  Pallas kernels: 30.6 us -> 27.9 us
    pallas_call x2, Pallas kernels: 16.6 us -> 13.9 us  [the longest x1 7.22 us: cross_spectrum(): pl.pallas_call(cross_kernel, in_specs=[pl.BlockSpec(memory_space=pltpu.SM...]
where the time goes in v5:
time: 109 us
  waiting for transfers between devices  50 us (46%)
  Pallas kernels  27.9 us (26%)
  starting transfers between devices  23.4 us (21%)
  local copies, waits for them, and re-layouts  6.32 us (6%)
    all_to_all x1, waiting for transfers between devices, per_device(): lax.all_to_all(harmonic.reshape(256, 24, 128), ('tracer', 'dev'), split_a...  34.6 us
    all_to_all x1, starting transfers between devices, per_device(): lax.all_to_all(harmonic.reshape(256, 24, 128), ('tracer', 'dev'), split_a...  12.4 us
    all_to_all x1, waiting for transfers between devices, per_device(): lax.all_to_all(folded, ('tracer', 'dev'), split_axis=0, concat_axis=0, ti...  12.4 us
    pallas_call x1, Pallas kernels, legendre_tables(): pl.pallas_call(legendre_kernel, in_specs=[smem, smem, smem, vmem, vmem, v...  12.2 us
    all_to_all x1, starting transfers between devices, per_device(): lax.all_to_all(folded, ('tracer', 'dev'), split_axis=0, concat_axis=0, ti...  8.64 us
    pallas_call x1, Pallas kernels, cross_spectrum(): pl.pallas_call(cross_kernel, in_specs=[pl.BlockSpec(memory_space=pltpu.SM...  7.22 us
    pallas_call x1, Pallas kernels, transform(): pl.pallas_call(transform_kernel, in_specs=[hbm, hbm], out_specs=pl.BlockS...  6.64 us
    unnamed x4, local copies, waits for them, and re-layouts  3.61 us
  transfers between devices with their start and end apart: 3, of which 3 were waited for; matrix products, arithmetic and copies ran while one was open for 2% of the time, Pallas kernels for 11%

profile of v5, /device:TPU:1, one launch (start us, length us, event | category | flops | bytes accessed | tf_op | source)
XLA Modules:
  0.0 109.1 jit_solution(12321775149610899532)
XLA Ops:
  0.0 0.0 copy-start
  0.0 0.9 broadcast_in_dim.43
  0.9 0.1 eq.57
  1.0 0.6 copy-done
  1.6 0.8 fusion.coef_ref
  2.4 1.9 %fold.1 = bf16[32,2,8,2048]{3,2,1,0:T(8,128)(2,1)} custom-call(bf16[2,256,2047]{2,1,0:T(8,128)(2,1)S(1)} %fusion.coef_ref), custom_call_target="tpu_custom_call" | custom-call | tf_op jit(solution)/shard_map/fold/pallas_call | solution.py:81
  4.2 8.6 %all-to-all-start = ((bf16[32,2,8,2048]{3,2,1,0:T(8,128)(2,1)}), bf16[32,2,8,2048]{3,2,1,0:T(8,128)(2,1)}, u32[]{:S(2)}, u32[]{:S(2)}) async-start(bf16[32,2,8,2048]{3,2,1,0:T(8,128)(2,1)} %fold.1), calls=%async_computation | async-start | bytes 4194304 | tf_op jit(solution)/shard_map/all_to_all | solution.py:419
  13.0 0.2 select_reduce_fusion
  13.2 0.1 divide_sqrt_fusion
  13.3 0.1 sqrt.21.a_ref
  13.4 0.1 sqrt.23
  13.5 0.1 floor_minimum_fusion
  13.6 12.2 %legendre.1.table_hbm = bf16[8,3840,128]{2,1,0:T(8,128)(2,1)S(1)} custom-call(s32[4]{0:T(128)S(1)} %get-tuple-element.6.start_ref, f32[6208]{0:T(1024)S(1)} %sqrt.21.a_ref, f32[6208]{0:T(1024)S(1)} %mul.194.ab_ref, f32[8,128]{1,0:T(8,128)S(1)} %get-tuple-element.20.cos_ref, f32[8,128]{1,0:T(8,128)S(1)} %get-tuple-element.19.weight_ref, ...), custom_call_target="tpu_custom_call" | custom-call | tf_op jit(solution)/shard_map/legendre/pallas_call | solution.py:160
  25.8 0.0 copy-start.1
  25.8 3.0 %copy-done.1 = bf16[8,3840,128]{2,1,0:T(8,128)(2,1)} copy-done((bf16[8,3840,128]{2,1,0:T(8,128)(2,1)}, bf16[8,3840,128]{2,1,0:T(8,128)(2,1)S(1)}, u32[]{:S(2)}) %copy-start.1) | copy-done | bytes 7864344
  28.9 12.4 %all-to-all-done = bf16[32,2,8,2048]{3,2,1,0:T(8,128)(2,1)} async-done(((bf16[32,2,8,2048]{3,2,1,0:T(8,128)(2,1)}), bf16[32,2,8,2048]{3,2,1,0:T(8,128)(2,1)}, u32[]{:S(2)}, u32[]{:S(2)}) %all-to-all-start) | async-done | bytes 2097184 | tf_op jit(solution)/shard_map/all_to_all | solution.py:419
  41.2 6.6 %transform.1 = bf16[6144,128]{1,0:T(8,128)(2,1)} custom-call(bf16[8,3840,128]{2,1,0:T(8,128)(2,1)} %copy-done.1, bf16[512,2048]{1,0:T(8,128)(2,1)} %bitcast.5.x_hbm), custom_call_target="tpu_custom_call" | custom-call | tf_op jit(solution)/shard_map/transform/pallas_call | solution.py:236
  47.9 12.4 %all-to-all-start.1 = ((bf16[256,24,128]{2,1,0:T(8,128)(2,1)}), bf16[256,24,128]{2,1,0:T(8,128)(2,1)}, u32[]{:S(2)}, u32[]{:S(2)}) async-start(bf16[256,24,128]{2,1,0:T(8,128)(2,1)} %bitcast.14), calls=%async_computation.1 | async-start | bytes 3145728 | tf_op jit(solution)/shard_map/all_to_all | solution.py:446
  60.3 1.5 %dynamic-slice_bitcast_fusion = bf16[6,512,256]{2,1,0:T(8,128)(2,1)S(1)} fusion(bf16[1,12,512,256]{3,2,1,0:T(8,128)(2,1)} %own_hbm.1, s32[]{:T(128)S(6)} %select_n.118), kind=kLoop, calls=%fused_computation.3 | loop fusion | bytes 3145732 | tf_op jit(solution)/shard_map/dynamic_slice | solution.py:415
  61.9 2.3 %collective-permute-start = (bf16[6,512,256]{2,1,0:T(8,128)(2,1)S(1)}, bf16[6,512,256]{2,1,0:T(8,128)(2,1)}, u32[]{:S(2)}, u32[]{:S(2)}) collective-permute-start(bf16[6,512,256]{2,1,0:T(8,128)(2,1)S(1)} %dynamic-slice_bitcast_fusion), channel_id=1, source_target_pairs={{0,128},{128,0},{1,129},{129,1},{2,130},{130,2},{3,131},{131,3},{4... | collective-permute-start | bytes 4718600 | tf_op jit(solution)/shard_map/ppermute | solution.py:416
  64.1 0.1 pad_add_fusion.who_ref
  64.2 3.1 %collective-permute-done.other_hbm = bf16[6,512,256]{2,1,0:T(8,128)(2,1)} collective-permute-done((bf16[6,512,256]{2,1,0:T(8,128)(2,1)S(1)}, bf16[6,512,256]{2,1,0:T(8,128)(2,1)}, u32[]{:S(2)}, u32[]{:S(2)}) %collective-permute-start) | collective-permute-done | bytes 1572896 | tf_op jit(solution)/shard_map/ppermute | solution.py:416
  67.3 34.6 %all-to-all-done.1 = bf16[256,24,128]{2,1,0:T(8,128)(2,1)} async-done(((bf16[256,24,128]{2,1,0:T(8,128)(2,1)}), bf16[256,24,128]{2,1,0:T(8,128)(2,1)}, u32[]{:S(2)}, u32[]{:S(2)}) %all-to-all-start.1) | async-done | bytes 1572896 | tf_op jit(solution)/shard_map/all_to_all | solution.py:446
  101.9 7.2 %cross.1 = f32[1,6,512,512]{3,2,1,0:T(8,128)} custom-call(s32[2]{0:T(128)S(1)} %pad_add_fusion.who_ref, bf16[6144,128]{1,0:T(8,128)(2,1)} %bitcast.7.harm_hbm, bf16[1,12,512,256]{3,2,1,0:T(8,128)(2,1)} %own_hbm.1, bf16[6,512,256]{2,1,0:T(8,128)(2,1)} %collective-permute-done.other_hbm), custom_call_target="tpu_custom_call" | custom-call | tf_op jit(solution)/shard_map/cross/pallas_call | solution.py:345
  (9 shorter events, 0.1 us)
Async XLA Ops:
  0.0 1.6 %copy-start = (bf16[1,2,256,2047]{2,1,3,0:T(2,128)(2,1)S(1)}, bf16[1,2,256,2047]{2,1,3,0:T(2,128)(2,1)}, u32[]{:S(2)}) copy-start(bf16[1,2,256,2047]{2,1,3,0:T(2,128)(2,1)} %param.3) | copy-start | bytes 6288388
  4.2 37.0 %all-to-all-start = ((bf16[32,2,8,2048]{3,2,1,0:T(8,128)(2,1)}), bf16[32,2,8,2048]{3,2,1,0:T(8,128)(2,1)}, u32[]{:S(2)}, u32[]{:S(2)}) async-start(bf16[32,2,8,2048]{3,2,1,0:T(8,128)(2,1)} %fold.1), calls=%async_computation | async-start | bytes 4194304 | tf_op jit(solution)/shard_map/all_to_all | solution.py:419
  25.8 3.0 %copy-start.1 = (bf16[8,3840,128]{2,1,0:T(8,128)(2,1)}, bf16[8,3840,128]{2,1,0:T(8,128)(2,1)S(1)}, u32[]{:S(2)}) copy-start(bf16[8,3840,128]{2,1,0:T(8,128)(2,1)S(1)} %legendre.1.table_hbm) | copy-start | bytes 23592964
  47.9 54.0 %all-to-all-start.1 = ((bf16[256,24,128]{2,1,0:T(8,128)(2,1)}), bf16[256,24,128]{2,1,0:T(8,128)(2,1)}, u32[]{:S(2)}, u32[]{:S(2)}) async-start(bf16[256,24,128]{2,1,0:T(8,128)(2,1)} %bitcast.14), calls=%async_computation.1 | async-start | bytes 3145728 | tf_op jit(solution)/shard_map/all_to_all | solution.py:446
  61.9 5.5 %collective-permute-start = (bf16[6,512,256]{2,1,0:T(8,128)(2,1)S(1)}, bf16[6,512,256]{2,1,0:T(8,128)(2,1)}, u32[]{:S(2)}, u32[]{:S(2)}) collective-permute-start(bf16[6,512,256]{2,1,0:T(8,128)(2,1)S(1)} %dynamic-slice_bitcast_fusion), channel_id=1, source_target_pairs={{0,128},{128,0},{1,129},{129,1},{2,130},{130,2},{3,131},{131,3},{4... | collective-permute-start | bytes 4718600 | tf_op jit(solution)/shard_map/ppermute | solution.py:416

commit v6 on v5

--- a/solution.py
+++ b/solution.py
@@ -281,7 +281,7 @@
 
 
 def cross_kernel(
-    who_ref, harm_hbm, own_hbm, other_hbm, out_hbm, harm, wide, own, other, out, sems
+    who_ref, harm_hbm, own_hbm, other_hbm, out_hbm, harm, wide, basis, out, sems
 ):
     tracer, owner = who_ref[0], who_ref[1]
     part = OWNERS * 24
@@ -291,10 +291,14 @@
         arrivals.append(pltpu.make_async_copy(harm_hbm.at[span], harm.at[span], sems.at[core]))
     for e in range(DEGREES):
         arrivals.append(
-            pltpu.make_async_copy(own_hbm.at[0, DEGREES * tracer + e], own.at[e], sems.at[2 + e])
+            pltpu.make_async_copy(
+                own_hbm.at[0, DEGREES * tracer + e], basis.at[tracer, e], sems.at[2 + e]
+            )
         )
         arrivals.append(
-            pltpu.make_async_copy(other_hbm.at[e], other.at[e], sems.at[2 + DEGREES + e])
+            pltpu.make_async_copy(
+                other_hbm.at[e], basis.at[1 - tracer, e], sems.at[2 + DEGREES + e]
+            )
         )
     for copy in arrivals:
         copy.start()
@@ -302,7 +306,6 @@
         arrivals[core].wait()
         span = pl.ds(core * part, part)
         wide[span, :] = harm[span, :].astype(jnp.float32)
-    first = tracer == 0
     tally = jnp.full((1, 512), owner + 1, jnp.int32).astype(jnp.float32)
     factor = 1.0 / jnp.sqrt(2.0 * tally)
     contract = (((1,), (1,)), ((), ()))
@@ -314,14 +317,11 @@
             arrivals[3 + 2 * e].wait()
         for e in group:
             fields = degree_fields(wide, e)
-            mine, theirs = own[e], other[e]
-            basis_lead = jnp.where(first, mine, theirs)
-            basis_trail = jnp.where(first, theirs, mine)
             lead = lax.dot_general(
-                basis_lead, fields[0], contract, preferred_element_type=jnp.float32
+                basis[0, e], fields[0], contract, preferred_element_type=jnp.float32
             )
             trail = lax.dot_general(
-                fields[1], basis_trail, contract, preferred_element_type=jnp.float32
+                fields[1], basis[1, e], contract, preferred_element_type=jnp.float32
             )
             total = jnp.dot(
                 lead.astype(jnp.bfloat16),
@@ -350,8 +350,7 @@
         scratch_shapes=[
             pltpu.VMEM((rows, 128), jnp.bfloat16),
             pltpu.VMEM((rows, 128), jnp.float32),
-            pltpu.VMEM((DEGREES, 512, 256), jnp.bfloat16),
-            pltpu.VMEM((DEGREES, 512, 256), jnp.bfloat16),
+            pltpu.VMEM((2, DEGREES, 512, 256), jnp.bfloat16),
             pltpu.VMEM((DEGREES, 512, 512), jnp.float32),
             pltpu.SemaphoreType.DMA((2 + 3 * DEGREES,)),
         ],

time: 109 us -> 109 us (level)
  no operation moved by 1% of the time
where the time goes in v6:
time: 109 us
  waiting for transfers between devices  50 us (46%)
  Pallas kernels  27.8 us (26%)
  starting transfers between devices  23.4 us (21%)
  local copies, waits for them, and re-layouts  6.32 us (6%)
    all_to_all x1, waiting for transfers between devices, per_device(): lax.all_to_all(harmonic.reshape(256, 24, 128), ('tracer', 'dev'), split_a...  34.6 us
    all_to_all x1, starting transfers between devices, per_device(): lax.all_to_all(harmonic.reshape(256, 24, 128), ('tracer', 'dev'), split_a...  12.4 us
    all_to_all x1, waiting for transfers between devices, per_device(): lax.all_to_all(folded, ('tracer', 'dev'), split_axis=0, concat_axis=0, ti...  12.4 us
    pallas_call x1, Pallas kernels, legendre_tables(): pl.pallas_call(legendre_kernel, in_specs=[smem, smem, smem, vmem, vmem, v...  12.2 us
    all_to_all x1, starting transfers between devices, per_device(): lax.all_to_all(folded, ('tracer', 'dev'), split_axis=0, concat_axis=0, ti...  8.64 us
    pallas_call x1, Pallas kernels, cross_spectrum(): pl.pallas_call(cross_kernel, in_specs=[pl.BlockSpec(memory_space=pltpu.SM...  7.13 us
    pallas_call x1, Pallas kernels, transform(): pl.pallas_call(transform_kernel, in_specs=[hbm, hbm], out_specs=pl.BlockS...  6.64 us
    unnamed x4, local copies, waits for them, and re-layouts  3.61 us
  transfers between devices with their start and end apart: 3, of which 3 were waited for; matrix products, arithmetic and copies ran while one was open for 2% of the time, Pallas kernels for 11%

profile of v6, /device:TPU:1, one launch (start us, length us, event | category | flops | bytes accessed | tf_op | source)
XLA Modules:
  0.0 109.0 jit_solution(11288180365777695685)
XLA Ops:
  0.0 0.0 copy-start
  0.0 0.9 broadcast_in_dim.43
  0.9 0.1 eq.57
  1.0 0.6 copy-done
  1.6 0.8 fusion.coef_ref
  2.4 1.9 %fold.1 = bf16[32,2,8,2048]{3,2,1,0:T(8,128)(2,1)} custom-call(bf16[2,256,2047]{2,1,0:T(8,128)(2,1)S(1)} %fusion.coef_ref), custom_call_target="tpu_custom_call" | custom-call | tf_op jit(solution)/shard_map/fold/pallas_call | solution.py:81
  4.2 8.6 %all-to-all-start = ((bf16[32,2,8,2048]{3,2,1,0:T(8,128)(2,1)}), bf16[32,2,8,2048]{3,2,1,0:T(8,128)(2,1)}, u32[]{:S(2)}, u32[]{:S(2)}) async-start(bf16[32,2,8,2048]{3,2,1,0:T(8,128)(2,1)} %fold.1), calls=%async_computation | async-start | bytes 4194304 | tf_op jit(solution)/shard_map/all_to_all | solution.py:418
  13.0 0.2 select_reduce_fusion
  13.2 0.1 divide_sqrt_fusion
  13.3 0.1 sqrt.21.a_ref
  13.4 0.1 sqrt.23
  13.5 0.1 floor_minimum_fusion
  13.6 12.2 %legendre.1.table_hbm = bf16[8,3840,128]{2,1,0:T(8,128)(2,1)S(1)} custom-call(s32[4]{0:T(128)S(1)} %get-tuple-element.6.start_ref, f32[6208]{0:T(1024)S(1)} %sqrt.21.a_ref, f32[6208]{0:T(1024)S(1)} %mul.194.ab_ref, f32[8,128]{1,0:T(8,128)S(1)} %get-tuple-element.20.cos_ref, f32[8,128]{1,0:T(8,128)S(1)} %get-tuple-element.19.weight_ref, ...), custom_call_target="tpu_custom_call" | custom-call | tf_op jit(solution)/shard_map/legendre/pallas_call | solution.py:160
  25.8 0.0 copy-start.1
  25.8 3.0 %copy-done.1 = bf16[8,3840,128]{2,1,0:T(8,128)(2,1)} copy-done((bf16[8,3840,128]{2,1,0:T(8,128)(2,1)}, bf16[8,3840,128]{2,1,0:T(8,128)(2,1)S(1)}, u32[]{:S(2)}) %copy-start.1) | copy-done | bytes 7864344
  28.9 12.4 %all-to-all-done = bf16[32,2,8,2048]{3,2,1,0:T(8,128)(2,1)} async-done(((bf16[32,2,8,2048]{3,2,1,0:T(8,128)(2,1)}), bf16[32,2,8,2048]{3,2,1,0:T(8,128)(2,1)}, u32[]{:S(2)}, u32[]{:S(2)}) %all-to-all-start) | async-done | bytes 2097184 | tf_op jit(solution)/shard_map/all_to_all | solution.py:418
  41.2 6.6 %transform.1 = bf16[6144,128]{1,0:T(8,128)(2,1)} custom-call(bf16[8,3840,128]{2,1,0:T(8,128)(2,1)} %copy-done.1, bf16[512,2048]{1,0:T(8,128)(2,1)} %bitcast.5.x_hbm), custom_call_target="tpu_custom_call" | custom-call | tf_op jit(solution)/shard_map/transform/pallas_call | solution.py:236
  47.9 12.4 %all-to-all-start.1 = ((bf16[256,24,128]{2,1,0:T(8,128)(2,1)}), bf16[256,24,128]{2,1,0:T(8,128)(2,1)}, u32[]{:S(2)}, u32[]{:S(2)}) async-start(bf16[256,24,128]{2,1,0:T(8,128)(2,1)} %bitcast.14), calls=%async_computation.1 | async-start | bytes 3145728 | tf_op jit(solution)/shard_map/all_to_all | solution.py:445
  60.3 1.5 %dynamic-slice_bitcast_fusion = bf16[6,512,256]{2,1,0:T(8,128)(2,1)S(1)} fusion(bf16[1,12,512,256]{3,2,1,0:T(8,128)(2,1)} %own_hbm.1, s32[]{:T(128)S(6)} %select_n.118), kind=kLoop, calls=%fused_computation.3 | loop fusion | bytes 3145732 | tf_op jit(solution)/shard_map/dynamic_slice | solution.py:414
  61.9 2.3 %collective-permute-start = (bf16[6,512,256]{2,1,0:T(8,128)(2,1)S(1)}, bf16[6,512,256]{2,1,0:T(8,128)(2,1)}, u32[]{:S(2)}, u32[]{:S(2)}) collective-permute-start(bf16[6,512,256]{2,1,0:T(8,128)(2,1)S(1)} %dynamic-slice_bitcast_fusion), channel_id=1, source_target_pairs={{0,128},{128,0},{1,129},{129,1},{2,130},{130,2},{3,131},{131,3},{4... | collective-permute-start | bytes 4718600 | tf_op jit(solution)/shard_map/ppermute | solution.py:415
  64.1 0.1 pad_add_fusion.who_ref
  64.2 3.1 %collective-permute-done.other_hbm = bf16[6,512,256]{2,1,0:T(8,128)(2,1)} collective-permute-done((bf16[6,512,256]{2,1,0:T(8,128)(2,1)S(1)}, bf16[6,512,256]{2,1,0:T(8,128)(2,1)}, u32[]{:S(2)}, u32[]{:S(2)}) %collective-permute-start) | collective-permute-done | bytes 1572896 | tf_op jit(solution)/shard_map/ppermute | solution.py:415
  67.3 34.6 %all-to-all-done.1 = bf16[256,24,128]{2,1,0:T(8,128)(2,1)} async-done(((bf16[256,24,128]{2,1,0:T(8,128)(2,1)}), bf16[256,24,128]{2,1,0:T(8,128)(2,1)}, u32[]{:S(2)}, u32[]{:S(2)}) %all-to-all-start.1) | async-done | bytes 1572896 | tf_op jit(solution)/shard_map/all_to_all | solution.py:445
  101.9 7.1 %cross.1 = f32[1,6,512,512]{3,2,1,0:T(8,128)} custom-call(s32[2]{0:T(128)S(1)} %pad_add_fusion.who_ref, bf16[6144,128]{1,0:T(8,128)(2,1)} %bitcast.7.harm_hbm, bf16[1,12,512,256]{3,2,1,0:T(8,128)(2,1)} %own_hbm.1, bf16[6,512,256]{2,1,0:T(8,128)(2,1)} %collective-permute-done.other_hbm), custom_call_target="tpu_custom_call" | custom-call | tf_op jit(solution)/shard_map/cross/pallas_call | solution.py:345
  (9 shorter events, 0.1 us)
Async XLA Ops:
  0.0 1.6 %copy-start = (bf16[1,2,256,2047]{2,1,3,0:T(2,128)(2,1)S(1)}, bf16[1,2,256,2047]{2,1,3,0:T(2,128)(2,1)}, u32[]{:S(2)}) copy-start(bf16[1,2,256,2047]{2,1,3,0:T(2,128)(2,1)} %param.3) | copy-start | bytes 6288388
  4.2 37.0 %all-to-all-start = ((bf16[32,2,8,2048]{3,2,1,0:T(8,128)(2,1)}), bf16[32,2,8,2048]{3,2,1,0:T(8,128)(2,1)}, u32[]{:S(2)}, u32[]{:S(2)}) async-start(bf16[32,2,8,2048]{3,2,1,0:T(8,128)(2,1)} %fold.1), calls=%async_computation | async-start | bytes 4194304 | tf_op jit(solution)/shard_map/all_to_all | solution.py:418
  25.8 3.0 %copy-start.1 = (bf16[8,3840,128]{2,1,0:T(8,128)(2,1)}, bf16[8,3840,128]{2,1,0:T(8,128)(2,1)S(1)}, u32[]{:S(2)}) copy-start(bf16[8,3840,128]{2,1,0:T(8,128)(2,1)S(1)} %legendre.1.table_hbm) | copy-start | bytes 23592964
  47.9 54.0 %all-to-all-start.1 = ((bf16[256,24,128]{2,1,0:T(8,128)(2,1)}), bf16[256,24,128]{2,1,0:T(8,128)(2,1)}, u32[]{:S(2)}, u32[]{:S(2)}) async-start(bf16[256,24,128]{2,1,0:T(8,128)(2,1)} %bitcast.14), calls=%async_computation.1 | async-start | bytes 3145728 | tf_op jit(solution)/shard_map/all_to_all | solution.py:445
  61.9 5.5 %collective-permute-start = (bf16[6,512,256]{2,1,0:T(8,128)(2,1)S(1)}, bf16[6,512,256]{2,1,0:T(8,128)(2,1)}, u32[]{:S(2)}, u32[]{:S(2)}) collective-permute-start(bf16[6,512,256]{2,1,0:T(8,128)(2,1)S(1)} %dynamic-slice_bitcast_fusion), channel_id=1, source_target_pairs={{0,128},{128,0},{1,129},{129,1},{2,130},{130,2},{3,131},{131,3},{4... | collective-permute-start | bytes 4718600 | tf_op jit(solution)/shard_map/ppermute | solution.py:415
